TPU v7x, 256 devices: a whole 4x4x8 slice. The times are simulated.
256 devices in a mesh: row: 8 (over x, core), col: 32 (over z, y).
Axes of the slice: x: 4, y: 4, z: 8, core: 2. Of those that a mesh axis runs over, the one named last changes fastest.
Arguments:
- source_pcs: bfloat16 [32768, 64], P('row'), may hold values from -8 to 8
- target_pcs: bfloat16 [131072, 64], P('col'), may hold values from -8 to 8
- source_mass: float32 [32768], P('row'), may hold values from 0.25 to 4
- target_mass: float32 [131072], P('col'), may hold values from 0.25 to 4
- source_scaling: float32 [32768], P('row'), may hold values from 0.1 to 10
- labels: int32 [131072], P('col'), may hold values from 0 to 31
Outputs:
- fates: float32 [32768, 32], P(('row', 'col'))
- source_potential: float32 [32768], P(('row', 'col'))
- target_potential: float32 [131072], P('col')
All inputs are finite; a program needn't handle non-finite values.
Results may differ from a plain program's by a relative error of at most 0.00035.
Values may be sent and summed in bfloat16 or wider, within the bound.
No kernel may reach another device: no remote copies, remote signals or barrier semaphores. Data moves between devices by JAX's collectives and lax.ppermute only.
A program may use at most 128 MiB of HBM per device.

v0:
```python
import jax
import jax.numpy as jnp
from jax import lax
from jax.sharding import PartitionSpec as P

SETS = 32
ITERS = 2


entropy_weight = 0.5
offset_small = 1e-06


def kernel_rows(source_pcs, source_sq, target_pcs, target_sq, inverse, first_row, row_count):
    source_block = lax.dynamic_slice_in_dim(source_pcs, first_row, row_count, 0)
    block_sq = lax.dynamic_slice_in_dim(source_sq, first_row, row_count, 0)
    inner_products = lax.dot_general(
        source_block, target_pcs, (((1,), (1,)), ((), ())), preferred_element_type=jnp.float32
    )
    exponent = (block_sq[:, None] + target_sq[None, :] - 2.0 * inner_products) * inverse
    return jnp.exp(-exponent).astype(jnp.bfloat16)


def on_device(source_pcs, target_pcs, source_mass, target_mass, source_scaling, labels):
    row_count = source_pcs.shape[0]
    col_count = target_pcs.shape[0]
    source_wide = source_pcs.astype(jnp.float32)
    target_wide = target_pcs.astype(jnp.float32)
    source_sq = jnp.sum(source_wide * source_wide, 1)
    target_sq = jnp.sum(target_wide * target_wide, 1)
    source_sum, source_sqsum = lax.psum((jnp.sum(source_wide, 0), jnp.sum(source_sq)), "row")
    target_sum, target_sqsum = lax.psum((jnp.sum(target_wide, 0), jnp.sum(target_sq)), "col")
    source_total = row_count * lax.axis_size("row")
    target_total = col_count * lax.axis_size("col")
    mean_square = (
        source_sqsum / source_total
        + target_sqsum / target_total
        - 2.0 * jnp.sum(source_sum / source_total * (target_sum / target_total))
        + offset_small
    )
    inverse = 1.0 / (entropy_weight * mean_square)
    block_rows = min(row_count, 512)
    block_count = row_count // block_rows

    def one_block(block_index):
        return kernel_rows(
            source_pcs,
            source_sq,
            target_pcs,
            target_sq,
            inverse,
            block_index * block_rows,
            block_rows,
        )

    kernel = lax.map(one_block, jnp.arange(block_count, dtype=jnp.int32)).reshape(
        row_count, col_count
    )

    def row_pass(right_side):
        return jnp.dot(kernel, right_side, preferred_element_type=jnp.float32)

    share_rows = row_count // lax.axis_size("col")
    own_first = lax.axis_index("col") * share_rows
    own_mass = lax.dynamic_slice_in_dim(source_mass, own_first, share_rows, 0)
    scaled = source_scaling.astype(jnp.bfloat16)
    target_scaling = target_mass
    for iteration in range(ITERS):
        column_sums = lax.psum(jnp.dot(scaled, kernel, preferred_element_type=jnp.float32), "row")
        target_scaling = target_mass / column_sums
        if iteration + 1 < ITERS:
            update_right_side = target_scaling.astype(jnp.bfloat16)
            row_sums = lax.psum(row_pass(update_right_side), "col")
            scaled = (source_mass / row_sums).astype(jnp.bfloat16)
    membership = labels[:, None] == jnp.arange(SETS, dtype=jnp.int32)[None, :]
    probes = jnp.where(
        membership, target_scaling.astype(jnp.bfloat16)[:, None], jnp.zeros((), jnp.bfloat16)
    )
    all_sums = lax.psum(row_pass(probes), "col")
    own_sums = lax.dynamic_slice_in_dim(all_sums, own_first, share_rows, 0)
    totals = jnp.sum(own_sums, 1)
    fates = own_sums / totals[:, None]
    source_potential = entropy_weight * jnp.log(own_mass / totals)
    target_potential = entropy_weight * jnp.log(target_scaling)
    return (fates, source_potential, target_potential)


def solution(mesh):
    placed = (P("row", None), P("col", None), P("row"), P("col"), P("row"), P("col"))
    return jax.shard_map(
        on_device,
        mesh=mesh,
        in_specs=placed,
        out_specs=(P(("row", "col"), None), P(("row", "col")), P("col")),
        check_vma=False,
    )
```

profile of v0, /device:TPU:1, one launch (start us, length us, event | category | flops | bytes accessed | tf_op | source)
XLA Modules:
  0.0 547.9 jit_solution(15440935241534829660)
XLA Ops:
  7.2 0.0 all-reduce.4.cloned.1.call-start
  7.2 2.2 convert_reduce_fusion
  9.5 15.6 %all-reduce.1 = (f32[]{:T(128)}, f32[64]{0:T(128)S(1)}) all-reduce(f32[]{:T(128)} %get-tuple-element.75, f32[64]{0:T(128)S(1)} %get-tuple-element.76), channel_id=1, replica_groups=mesh['row'=8,'col'=32] {'row'}, use_global_device_ids=true, to_apply=%region_3.0 | all-reduce | flops 65 | bytes 520 | tf_op jit(solution)/shard_map/psum | solution.py:31
  25.7 63.0 %all-reduce = (f32[]{:T(128)}, f32[64]{0:T(128)S(1)}) all-reduce(f32[]{:T(128)} %get-tuple-element.50, f32[64]{0:T(128)S(1)} %get-tuple-element.49), channel_id=1, replica_groups=mesh['row'=8,'col'=32] {'col'}, use_global_device_ids=true, to_apply=%region_5.0 | all-reduce | flops 65 | bytes 520 | tf_op jit(solution)/shard_map/psum | solution.py:32
  89.4 0.6 multiply_reduce_fusion
  90.7 0.0 copy-start.3
  90.7 52.0 %while.10 = (s32[]{:T(128)}, bf16[8,512,4096]{2,1,0:T(8,128)(2,1)}, s32[8]{0:T(128)S(1)}, f32[4096]{0:T(1024)S(1)}, f32[4096]{0:T(1024)S(1)}, /*index=5*/bf16[40...) while((s32[]{:T(128)}, bf16[8,512,4096]{2,1,0:T(8,128)(2,1)}, ...), condition=%wide.region_12.13_spmd, body=%wide.region_11.12_spmd.sunk | while | flops 281018368 | bytes 4807863 | solution.py:56
  90.7 0.6 dynamic_slice.29
  91.9 0.1 dynamic_slice.30
  92.0 5.1 fusion.31
  97.2 0.6 dynamic_slice.29
  98.4 0.1 dynamic_slice.30
  98.5 5.2 fusion.31
  103.7 0.6 dynamic_slice.29
  104.9 0.1 dynamic_slice.30
  105.0 5.2 fusion.31
  110.2 0.6 dynamic_slice.29
  111.4 0.1 dynamic_slice.30
  111.5 5.2 fusion.31
  116.7 0.6 dynamic_slice.29
  117.9 0.1 dynamic_slice.30
  118.0 5.1 fusion.31
  123.2 0.6 dynamic_slice.29
  124.4 0.1 dynamic_slice.30
  124.5 5.2 fusion.31
  129.7 0.6 dynamic_slice.29
  130.9 0.1 dynamic_slice.30
  131.0 5.2 fusion.31
  136.2 0.6 dynamic_slice.29
  137.4 0.1 dynamic_slice.30
  137.5 5.2 fusion.31
  142.7 0.0 copy-done.3
  142.7 0.0 copy-start
  142.7 0.0 copy-start.1
  142.7 12.8 %fusion.15 = f32[1,4096]{1,0:T(1,128)S(1)} fusion(bf16[4096,4096]{1,0:T(8,128)(2,1)} %bitcast.23, bf16[4096,1]{0,1:T(2,128)(2,1)S(1)} %reshape.17), kind=kOutput, calls=%fused_computation.29 | convolution fusion | flops 33554432 | bytes 33579008 | tf_op jit(solution)/shard_map/dot_general | solution.py:69
  155.6 36.8 %psum.60 = f32[4096]{0:T(1024)S(1)} all-reduce(f32[4096]{0:T(1024)S(1)} %bitcast.28), channel_id=1, replica_groups=mesh['row'=8,'col'=32] {'row'}, use_global_device_ids=true, to_apply=%region_13.14 | all-reduce | flops 4096 | bytes 32768 | tf_op jit(solution)/shard_map/psum | solution.py:69
  192.3 0.0 copy-done
  192.4 0.0 copy-start.2
  192.4 15.0 %fusion.16 = f32[1,4096]{1,0:T(1,128)S(1)} fusion(bf16[4096,4096]{1,0:T(8,128)(2,1)} %bitcast.24, bf16[4096,1]{0,1:T(2,128)(2,1)S(1)} %reshape.19), kind=kOutput, calls=%fused_computation.30 | convolution fusion | flops 33554432 | bytes 33579008 | tf_op jit(solution)/shard_map/dot_general | solution.py:61
  207.4 110.4 %psum.61 = f32[4096]{0:T(1024)S(1)} all-reduce(f32[4096]{0:T(1024)S(1)} %bitcast.27), channel_id=1, replica_groups=mesh['row'=8,'col'=32] {'col'}, use_global_device_ids=true, to_apply=%region_14.15 | all-reduce | flops 4096 | bytes 32768 | tf_op jit(solution)/shard_map/psum | solution.py:73
  317.7 0.0 copy-done.1
  317.8 12.8 %fusion.17 = f32[1,4096]{1,0:T(1,128)S(1)} fusion(bf16[4096,1]{0,1:T(2,128)(2,1)S(1)} %reshape.21, bf16[4096,4096]{1,0:T(8,128)(2,1)} %bitcast.25), kind=kOutput, calls=%fused_computation.31 | convolution fusion | flops 33554432 | bytes 33579008 | tf_op jit(solution)/shard_map/dot_general | solution.py:69
  330.6 51.0 %psum.62 = f32[4096]{0:T(1024)S(1)} all-reduce(f32[4096]{0:T(1024)S(1)} %bitcast.29), channel_id=1, replica_groups=mesh['row'=8,'col'=32] {'row'}, use_global_device_ids=true, to_apply=%region_15.16 | all-reduce | flops 4096 | bytes 32768 | tf_op jit(solution)/shard_map/psum | solution.py:69
  381.6 0.6 log_multiply_fusion
  382.3 0.0 copy-done.2
  382.3 16.6 %fusion.9 = f32[4096,32]{0,1:T(8,128)} fusion(bf16[4096,4096]{1,0:T(8,128)(2,1)} %bitcast.26, s32[4096]{0:T(1024)S(1)} %copy-done.2, bf16[4096]{0:T(1024)(128)(2,1)S(1)} %get-tuple-element.73), kind=kOutput, calls=%fused_computation.15 | convolution fusion | flops 1074003968 | bytes 34103296 | tf_op jit(solution)/shard_map/dot_general | solution.py:61
  398.9 0.0 all-reduce.4.cloned.1.call-update
  398.9 139.5 %all-reduce.4.cloned.1.call-done = f32[4096,32]{0,1:T(8,128)} async-done(((f32[4096,32]{0,1:T(8,128)}), f32[4096,32]{0,1:T(8,128)}) %all-reduce.4.cloned.1.call-update) | async-done | bytes 524304 | tf_op jit(solution)/shard_map/psum | solution.py:79
  538.4 0.7 dynamic-slice_reduce_fusion
  539.2 0.6 log_multiply_fusion.1
  539.8 1.3 dynamic-slice_divide_fusion
  (8 shorter events, 0.1 us)
Async XLA Ops:
  7.2 531.3 %all-reduce.4.cloned.1.call-start = ((), (), s32[]{:S(2)}) async-start(), calls=%async_computation | async-start | bytes 1048576 | tf_op jit(solution)/shard_map/psum | solution.py:79
  90.7 52.0 %copy-start.3 = (f32[4096]{0:T(1024)S(1)}, f32[4096]{0:T(1024)}, u32[]{:S(2)}) copy-start(f32[4096]{0:T(1024)} %param.12) | copy-start | bytes 49156
  142.7 49.7 %copy-start = (f32[4096]{0:T(1024)S(1)}, f32[4096]{0:T(1024)}, u32[]{:S(2)}) copy-start(f32[4096]{0:T(1024)} %param.11) | copy-start | bytes 49156
  142.7 175.0 %copy-start.1 = (f32[4096]{0:T(1024)S(1)}, f32[4096]{0:T(1024)}, u32[]{:S(2)}) copy-start(f32[4096]{0:T(1024)} %param.10) | copy-start | bytes 49156
  192.4 189.9 %copy-start.2 = (s32[4096]{0:T(1024)S(1)}, s32[4096]{0:T(1024)}, u32[]{:S(2)}) copy-start(s32[4096]{0:T(1024)} %param.13) | copy-start | bytes 49156
Sparse Core Ops, SparseCore 0:
  399.0 139.3 all-reduce.3
where the time goes:
time: 552 us; the launch traced here: 548 us
  blocking collectives  277 us (50%)
  waiting for transfers between devices  140 us (25%)
  matrix products  98.7 us (18%)
  between operations  16.1 us (3%)
  other arithmetic  6.15 us (1%)
    psum x1, waiting for transfers between devices, on_device(): all_sums = lax.psum(row_pass(probes), 'col')  140 us
    psum x1, blocking collectives, on_device(): row_sums = lax.psum(row_pass(update_right_side), 'col')  110 us
    psum x2, blocking collectives, on_device(): lax.psum(jnp.dot(scaled, kernel, preferred_element_type=jnp.float32), 'row')  87.8 us
    psum x1, blocking collectives, on_device(): lax.psum((jnp.sum(target_wide, 0), jnp.sum(target_sq)), 'col')  63 us
    dot_general x8, matrix products, kernel_rows(): lax.dot_general(source_block, target_pcs, (((1,), (1,)), ((), ())), prefe...  41.5 us
    dot_general x2, matrix products, row_pass(): return jnp.dot(kernel, right_side, preferred_element_type=jnp.float32)  31.6 us
    dot_general x2, matrix products, on_device(): jnp.dot(scaled, kernel, preferred_element_type=jnp.float32)  25.7 us
    psum x1, blocking collectives, on_device(): lax.psum((jnp.sum(source_wide, 0), jnp.sum(source_sq)), 'row')  15.6 us
  transfers between devices with their start and end apart: 1, of which 1 were waited for; matrix products, arithmetic and copies ran while one was open for 0% of the time, Pallas kernels for 0%

commit v1 on v0

v1 whole, which is shorter than its diff:
```python
import functools

import jax
import jax.numpy as jnp
import numpy as np
from jax import lax
from jax.experimental import pallas as pl
from jax.experimental.pallas import tpu as pltpu
from jax.sharding import PartitionSpec as P

SETS = 32
PCS = 64
LANES = 128
DEPTH = 128
entropy_weight = 0.5
offset_small = 1e-06
LOG2E = 1.4426950408889634
F32 = jnp.float32
BF16 = jnp.bfloat16
NT_DIMS = (((1,), (1,)), ((), ()))
VMEM = pl.BlockSpec(memory_space=pltpu.VMEM)
SMEM = pl.BlockSpec(memory_space=pltpu.SMEM)


def split3(t):
    hi = t.astype(BF16).astype(F32)
    mid = (t - hi).astype(BF16).astype(F32)
    lo = t - hi - mid
    return hi, mid, lo


def prep_kernel(peers, x_ref, y_ref, xa_ref, ya_ref, stats_ref):
    rows = 512
    lane = lax.broadcasted_iota(jnp.int32, (rows, LANES - PCS), 1)
    for which, (in_ref, out_ref) in enumerate(((x_ref, xa_ref), (y_ref, ya_ref))):
        total = jnp.zeros((1, PCS), F32)
        total_sq = jnp.zeros((1, 1), F32)
        for first in range(0, in_ref.shape[0], rows):
            part = in_ref[first : first + rows, :]
            wide = part.astype(F32)
            sq = jnp.sum(wide * wide, 1, keepdims=True)
            total = total + jnp.sum(wide, 0, keepdims=True)
            total_sq = total_sq + jnp.sum(sq, 0, keepdims=True)
            parts = split3(-0.5 * sq)
            base = 3 * which
            extra = jnp.where((lane >= 3 - base) & (lane < 6 - base), 1.0, 0.0)
            for k in range(3):
                extra = jnp.where(lane == base + k, parts[k], extra)
            out_ref[first : first + rows, 0:PCS] = part
            out_ref[first : first + rows, PCS:LANES] = extra.astype(BF16)
        for peer in range(peers):
            stats_ref[peer, which : which + 1, 0:PCS] = total
            stats_ref[peer, which : which + 1, PCS:LANES] = jnp.broadcast_to(
                total_sq, (1, LANES - PCS)
            )


def gen_kernel(peers, weight_x, weight_y, xa_ref, ya_ref, stats_ref, scaling_ref, k_ref, out_ref):
    row_count, col_count = xa_ref.shape[0], ya_ref.shape[0]
    sums = jnp.sum(stats_ref[...], 0)
    mean_x = sums[0:1, :] * weight_x
    mean_y = sums[1:2, :] * weight_y
    lane = lax.broadcasted_iota(jnp.int32, (1, LANES), 1)
    square = jnp.where(lane == PCS, mean_x + mean_y, 0.0)
    cross = jnp.where(lane < PCS, mean_x * mean_y, 0.0)
    mean_square = jnp.sum(square - 2.0 * cross, 1, keepdims=True) + offset_small
    factor = (2.0 * LOG2E) / (entropy_weight * mean_square)
    block_cols, block_rows = 512, 256

    def one_block(index, carry):
        first = pl.multiple_of(index * block_cols, block_cols)
        acc = None
        for row in range(0, row_count, block_rows):
            inner = lax.dot_general(
                ya_ref[pl.ds(first, block_cols), :],
                xa_ref[row : row + block_rows, :],
                NT_DIMS,
                preferred_element_type=F32,
            )
            value = jnp.exp2(inner * factor)
            k_ref[pl.ds(first, block_cols), row : row + block_rows] = value.astype(BF16)
            for part in range(0, block_rows, LANES):
                at = (row + part) // LANES
                scaled = scaling_ref[at : at + 1, :].astype(BF16).astype(F32)
                term = value[:, part : part + LANES] * scaled
                acc = term if acc is None else acc + term
        for part in range(0, block_cols, LANES):
            line = jnp.sum(acc[part : part + LANES, :].T, 0, keepdims=True)
            for peer in range(peers):
                out_ref[peer, pl.ds(index * (block_cols // LANES) + part // LANES, 1), :] = line
        return carry

    lax.fori_loop(0, col_count // block_cols, one_block, 0)


def spread(ref, values):
    for t in range(values.shape[0]):
        ref[:, t * LANES : (t + 1) * LANES] = jnp.broadcast_to(
            values[t : t + 1, :], (ref.shape[0], LANES)
        ).astype(BF16)


def row_kernel(peers, k_ref, sums_ref, mass_ref, out_ref, left_ref, line_ref):
    spread(left_ref, mass_ref[...] / jnp.sum(sums_ref[...], 0))
    count = k_ref.shape[1]
    block = 512
    for first in range(0, count, block):
        result = jnp.dot(
            left_ref[...], k_ref[:, first : first + block], preferred_element_type=F32
        )
        for part in range(0, block, LANES):
            at = (first + part) // LANES
            line_ref[at : at + 1, :] = result[0:1, part : part + LANES]
    whole = line_ref[...]
    for peer in range(peers):
        out_ref[peer] = whole


def col_kernel(peers, k_ref, sums_ref, mass_ref, out_ref, left_ref, line_ref):
    spread(left_ref, mass_ref[...] / jnp.sum(sums_ref[...], 0))
    count = k_ref.shape[0]
    block = 512
    for first in range(0, count, block):
        result = lax.dot_general(
            left_ref[...],
            k_ref[first : first + block, :],
            NT_DIMS,
            preferred_element_type=F32,
        )
        for part in range(0, block, LANES):
            at = (first + part) // LANES
            line_ref[at : at + 1, :] = result[0:1, part : part + LANES]
    whole = line_ref[...]
    for peer in range(peers):
        out_ref[peer] = whole


def fate_kernel(k_ref, sums_ref, mass_ref, labels_ref, out_ref, potential_ref, left_ref):
    scaling = mass_ref[...] / jnp.sum(sums_ref[...], 0)
    potential_ref[...] = entropy_weight * jnp.log(scaling)
    sets = lax.broadcasted_iota(jnp.int32, (SETS, LANES), 0)
    for t in range(scaling.shape[0]):
        member = labels_ref[t : t + 1, :] == sets
        left_ref[:, t * LANES : (t + 1) * LANES] = jnp.where(
            member, scaling[t : t + 1, :], 0.0
        ).astype(BF16)
    count = k_ref.shape[1]
    block = 512
    for first in range(0, count, block):
        result = jnp.dot(
            left_ref[...], k_ref[:, first : first + block], preferred_element_type=F32
        )
        for part in range(0, block, LANES):
            out_ref[(first + part) // LANES] = result[:, part : part + LANES]


def last_kernel(at_ref, sums_ref, mass_ref, fates_ref, potential_ref):
    sums = jnp.sum(sums_ref[...], 0)
    totals = jnp.sum(sums, 0, keepdims=True)
    fates_ref[...] = (sums / totals).T
    own = mass_ref[pl.ds(at_ref[0], 1), :]
    potential_ref[...] = entropy_weight * jnp.log(own / totals)


def shape(dims, dtype=F32):
    return jax.ShapeDtypeStruct(dims, dtype)


def call(kernel, name, outs, in_specs, scratch=(), limit=24):
    return pl.pallas_call(
        kernel,
        name=name,
        out_shape=outs,
        in_specs=in_specs,
        out_specs=tuple(VMEM for _ in outs) if isinstance(outs, tuple) else VMEM,
        scratch_shapes=scratch,
        compiler_params=pltpu.CompilerParams(vmem_limit_bytes=limit * 2**20),
    )


def diagonal_groups(row_size, col_size):
    groups = []
    for g in range(row_size):
        group = []
        for c in range(col_size):
            x = (g // 2 + c // 4) % (row_size // 2)
            core = (g % 2 + c % 4) % 2
            group.append((x * 2 + core) * col_size + c)
        groups.append(group)
    return groups


def on_device(row_size, col_size, source_pcs, target_pcs, source_mass, target_mass, source_scaling, labels):
    row_count = source_pcs.shape[0]
    col_count = target_pcs.shape[0]
    lines_r, lines_c = row_count // LANES, col_count // LANES
    source_mass = source_mass.reshape(lines_r, LANES)
    target_mass = target_mass.reshape(lines_c, LANES)
    scaling = source_scaling.reshape(lines_r, LANES)
    labels = labels.reshape(lines_c, LANES)

    xa, ya, stats = call(
        functools.partial(prep_kernel, col_size),
        "prep",
        (
            shape((row_count, DEPTH), BF16),
            shape((col_count, DEPTH), BF16),
            shape((col_size, 2, LANES)),
        ),
        [VMEM] * 2,
    )(source_pcs, target_pcs)
    stats = lax.all_to_all(
        stats, ("row", "col"), 0, 0,
        axis_index_groups=diagonal_groups(row_size, col_size), tiled=True,
    )
    repeats = col_size // row_size
    k, sums = call(
        functools.partial(
            gen_kernel,
            row_size,
            1.0 / (repeats * row_count * row_size),
            1.0 / (col_count * col_size),
        ),
        "gen",
        (pltpu.VMEM((col_count, row_count), BF16), shape((row_size, lines_c, LANES))),
        [VMEM] * 4,
    )(xa, ya, stats, scaling)
    k = pltpu.with_memory_space_constraint(k, pltpu.VMEM)
    sums = lax.all_to_all(sums, "row", 0, 0, tiled=True)
    scratch = [pltpu.VMEM((16, col_count), BF16), pltpu.VMEM((lines_r, LANES), F32)]
    sums = call(
        functools.partial(row_kernel, col_size),
        "rows",
        shape((col_size, lines_r, LANES)),
        [VMEM] * 3,
        scratch,
    )(k, sums, target_mass)
    sums = lax.all_to_all(sums, "col", 0, 0, tiled=True)
    scratch = [pltpu.VMEM((16, row_count), BF16), pltpu.VMEM((lines_c, LANES), F32)]
    sums = call(
        functools.partial(col_kernel, row_size),
        "cols",
        shape((row_size, lines_c, LANES)),
        [VMEM] * 3,
        scratch,
    )(k, sums, source_mass)
    sums = lax.all_to_all(sums, "row", 0, 0, tiled=True)
    sums, target_potential = call(
        fate_kernel,
        "fate",
        (shape((lines_r, SETS, LANES)), shape((lines_c, LANES))),
        [VMEM] * 4,
        [pltpu.VMEM((SETS, col_count), BF16)],
    )(k, sums, target_mass, labels)
    sums = lax.all_to_all(sums, "col", 0, 0, tiled=True)
    at = lax.axis_index("col").astype(jnp.int32).reshape(1)
    fates, source_potential = call(
        last_kernel,
        "last",
        (shape((LANES, SETS)), shape((1, LANES))),
        [SMEM, VMEM, VMEM],
    )(at, sums, source_mass)
    return fates, source_potential.reshape(LANES), target_potential.reshape(col_count)


def solution(mesh):
    placed = (P("row", None), P("col", None), P("row"), P("col"), P("row"), P("col"))
    return jax.shard_map(
        functools.partial(on_device, mesh.shape["row"], mesh.shape["col"]),
        mesh=mesh,
        in_specs=placed,
        out_specs=(P(("row", "col"), None), P(("row", "col")), P("col")),
        check_vma=False,
    )
```

time: 552 us -> 138 us (0.25)
  blocking collectives: 277 us -> 66.6 us
  waiting for transfers between devices: 140 us -> 15.5 us
  matrix products: 98.7 us -> 0 us
  Pallas kernels: 0 us -> 42.9 us
  between operations: 16.1 us -> 0.67 us
  other arithmetic: 6.15 us -> 0 us
    psum x5 -> x0, blocking collectives: 277 us -> none  [the longest x1 110 us: on_device(): row_sums = lax.psum(row_pass(update_right_side), 'col')]
    psum x1 -> x0, waiting for transfers between devices: 140 us -> none  [on_device(): all_sums = lax.psum(row_pass(probes), 'col')]
    dot_general x12 -> x0, matrix products: 98.7 us -> none  [the longest x8 41.5 us: kernel_rows(): lax.dot_general(source_block, target_pcs, (((1,), (1,)), ((), ())), prefe...]
    all_to_all x0 -> x4, blocking collectives: none -> 66.6 us  [the longest x1 24.1 us: on_device(): lax.all_to_all(stats, ('row', 'col'), 0, 0, axis_index_groups=diagonal_gr...]
    pallas_call x0 -> x6, Pallas kernels: none -> 42.9 us  [the longest x1 14.9 us: on_device(): call(functools.partial(gen_kernel, row_size, 1.0 / (repeats * row_count *...]
    all_to_all x0 -> x1, waiting for transfers between devices: none -> 15.5 us  [on_device(): sums = lax.all_to_all(sums, 'col', 0, 0, tiled=True)]
    unnamed x8 -> x9, local copies, waits for them, and re-layouts: 0.02 us -> 5.71 us
where the time goes in v1:
time: 138 us; the launch traced here: 136 us
  blocking collectives  66.6 us (48%)
  Pallas kernels  42.9 us (31%)
  waiting for transfers between devices  15.5 us (11%)
  local copies, waits for them, and re-layouts  5.71 us (4%)
  starting transfers between devices  4.39 us (3%)
    all_to_all x1, blocking collectives, on_device(): lax.all_to_all(stats, ('row', 'col'), 0, 0, axis_index_groups=diagonal_gr...  24.1 us
    all_to_all x2, blocking collectives, on_device(): sums = lax.all_to_all(sums, 'row', 0, 0, tiled=True)  21.6 us
    all_to_all x1, blocking collectives, on_device(): sums = lax.all_to_all(sums, 'col', 0, 0, tiled=True)  20.9 us
    all_to_all x1, waiting for transfers between devices, on_device(): sums = lax.all_to_all(sums, 'col', 0, 0, tiled=True)  15.5 us
    pallas_call x1, Pallas kernels, on_device(): call(functools.partial(gen_kernel, row_size, 1.0 / (repeats * row_count *...  14.9 us
    pallas_call x1, Pallas kernels, on_device(): call(functools.partial(col_kernel, row_size), 'cols', shape((row_size, li...  10.5 us
    pallas_call x1, Pallas kernels, on_device(): call(fate_kernel, 'fate', (shape((lines_r, SETS, LANES)), shape((lines_c,...  7.66 us
    pallas_call x1, Pallas kernels, on_device(): call(functools.partial(row_kernel, col_size), 'rows', shape((col_size, li...  6.19 us
  transfers between devices with their start and end apart: 1, of which 1 were waited for; matrix products, arithmetic and copies ran while one was open for 0% of the time, Pallas kernels for 0%

profile of v1, /device:TPU:1, one launch (start us, length us, event | category | flops | bytes accessed | tf_op | source)
XLA Modules:
  0.0 135.8 jit_solution(5722986469236448269)
XLA Ops:
  0.6 1.5 %copy.10.y_ref = bf16[4096,64]{1,0:T(8,128)(2,1)S(1)} copy(bf16[4096,64]{0,1:T(8,128)(2,1)} %param.7) | data formatting | bytes 1048576 | tf_op args[1]
  2.2 1.5 %copy.9.x_ref = bf16[4096,64]{1,0:T(8,128)(2,1)S(1)} copy(bf16[4096,64]{0,1:T(8,128)(2,1)} %param.6) | data formatting | bytes 1048576 | tf_op args[0]
  3.7 3.2 %prep.1 = (bf16[4096,128]{1,0:T(8,128)(2,1)S(1)}, bf16[4096,128]{1,0:T(8,128)(2,1)S(1)}, f32[32,2,128]{2,1,0:T(2,128)S(1)}) custom-call(bf16[4096,64]{1,0:T(8,128)(2,1)S(1)} %copy.9.x_ref, bf16[4096,64]{1,0:T(8,128)(2,1)S(1)} %copy.10.y_ref), custom_call_target="tpu_custom_call" | custom-call | tf_op jit(solution)/shard_map/prep/pallas_call | solution.py:202
  6.9 0.0 copy-start
  6.9 1.0 copy-done
  7.8 0.0 copy-start.1
  7.8 1.0 copy-done.1
  8.9 24.1 %all_to_all.25.stats_ref = f32[32,2,128]{2,1,0:T(2,128)} all-to-all(f32[32,2,128]{2,1,0:T(2,128)S(1)} %get-tuple-element.14), channel_id=1, replica_groups={{0,33,2,35,68,101,70,103,136,169,138,171,204,237,206,239,16,49,18,51,84..., dimensions={0} | all-to-all | bytes 65536 | tf_op jit(solution)/shard_map/all_to_all | solution.py:212
  33.0 14.9 %gen.1 = (bf16[4096,4096]{1,0:T(8,128)(2,1)S(1)}, f32[8,32,128]{2,1,0:T(8,128)}) custom-call(bf16[4096,128]{1,0:T(8,128)(2,1)} %copy-done, bf16[4096,128]{1,0:T(8,128)(2,1)} %copy-done.1, f32[32,2,128]{2,1,0:T(2,128)} %all_to_all.25.stats_ref, f32[32,128]{1,0:T(8,128)} %bitcast.12), custom_call_target="tpu_custom_call" | custom-call | tf_op jit(solution)/shard_map/gen/pallas_call | solution.py:217
  47.9 10.0 %all_to_all.26.sums_ref = f32[8,32,128]{2,1,0:T(8,128)} all-to-all(f32[8,32,128]{2,1,0:T(8,128)} %get-tuple-element.16), channel_id=1, replica_groups=mesh['row'=8,'col'=32] {'row'}, dimensions={0} | all-to-all | bytes 262144 | tf_op jit(solution)/shard_map/all_to_all | solution.py:229
  57.9 6.2 %rows.1 = f32[32,32,128]{2,1,0:T(8,128)} custom-call(bf16[4096,4096]{1,0:T(8,128)(2,1)S(1)} %get-tuple-element.15.k_ref, f32[8,32,128]{2,1,0:T(8,128)} %all_to_all.26.sums_ref, f32[32,128]{1,0:T(8,128)} %bitcast.9), custom_call_target="tpu_custom_call" | custom-call | tf_op jit(solution)/shard_map/rows/pallas_call | solution.py:231
  64.0 20.9 %all_to_all.27.sums_ref = f32[32,32,128]{2,1,0:T(8,128)} all-to-all(f32[32,32,128]{2,1,0:T(8,128)} %rows.1), channel_id=1, replica_groups=mesh['row'=8,'col'=32] {'col'}, dimensions={0} | all-to-all | bytes 1048576 | tf_op jit(solution)/shard_map/all_to_all | solution.py:238
  84.9 0.0 copy-start.2
  84.9 10.5 %cols.1 = f32[8,32,128]{2,1,0:T(8,128)} custom-call(bf16[4096,4096]{1,0:T(8,128)(2,1)S(1)} %get-tuple-element.15.k_ref, f32[32,32,128]{2,1,0:T(8,128)} %all_to_all.27.sums_ref, f32[32,128]{1,0:T(8,128)} %bitcast.7), custom_call_target="tpu_custom_call" | custom-call | tf_op jit(solution)/shard_map/cols/pallas_call | solution.py:240
  95.4 11.6 %all_to_all.28.sums_ref = f32[8,32,128]{2,1,0:T(8,128)} all-to-all(f32[8,32,128]{2,1,0:T(8,128)} %cols.1), channel_id=1, replica_groups=mesh['row'=8,'col'=32] {'row'}, dimensions={0} | all-to-all | bytes 262144 | tf_op jit(solution)/shard_map/all_to_all | solution.py:247
  107.0 7.7 %fate.1 = (f32[32,32,128]{2,1,0:T(8,128)}, f32[32,128]{1,0:T(8,128)}) custom-call(bf16[4096,4096]{1,0:T(8,128)(2,1)S(1)} %get-tuple-element.15.k_ref, f32[8,32,128]{2,1,0:T(8,128)} %all_to_all.28.sums_ref, f32[32,128]{1,0:T(8,128)} %bitcast.10, s32[32,128]{1,0:T(8,128)} %bitcast.11), custom_call_target="tpu_custom_call" | custom-call | tf_op jit(solution)/shard_map/fate/pallas_call | solution.py:248
  114.6 4.4 %all-to-all-start.4 = ((f32[32,32,128]{2,1,0:T(8,128)}), f32[32,32,128]{2,1,0:T(8,128)S(1)}, u32[]{:S(2)}, u32[]{:S(2)}) async-start(f32[32,32,128]{2,1,0:T(8,128)} %get-tuple-element.17), calls=%async_computation.4 | async-start | bytes 1048576 | tf_op jit(solution)/shard_map/all_to_all | solution.py:255
  119.0 15.5 %all-to-all-done.4.sums_ref = f32[32,32,128]{2,1,0:T(8,128)S(1)} async-done(((f32[32,32,128]{2,1,0:T(8,128)}), f32[32,32,128]{2,1,0:T(8,128)S(1)}, u32[]{:S(2)}, u32[]{:S(2)}) %all-to-all-start.4) | async-done | bytes 524320 | tf_op jit(solution)/shard_map/all_to_all | solution.py:255
  134.5 0.0 copy-done.2
  134.5 0.6 last.1
  135.1 0.7 copy.11
Async XLA Ops:
  6.9 1.0 copy-start
  7.8 1.0 copy-start.1
  84.9 49.6 %copy-start.2 = (f32[4096]{0:T(1024)S(1)}, f32[4096]{0:T(1024)}, u32[]{:S(2)}) copy-start(f32[4096]{0:T(1024)} %param.8) | copy-start | bytes 49156
  114.6 19.9 %all-to-all-start.4 = ((f32[32,32,128]{2,1,0:T(8,128)}), f32[32,32,128]{2,1,0:T(8,128)S(1)}, u32[]{:S(2)}, u32[]{:S(2)}) async-start(f32[32,32,128]{2,1,0:T(8,128)} %get-tuple-element.17), calls=%async_computation.4 | async-start | bytes 1048576 | tf_op jit(solution)/shard_map/all_to_all | solution.py:255

commit v2 on v1

--- a/solution.py
+++ b/solution.py
@@ -29,30 +29,38 @@
     return hi, mid, lo
 
 
-def prep_kernel(peers, x_ref, y_ref, xa_ref, ya_ref, stats_ref):
-    rows = 512
-    lane = lax.broadcasted_iota(jnp.int32, (rows, LANES - PCS), 1)
+def stats_kernel(peers, x_ref, y_ref, out_ref):
+    for which, in_ref in enumerate((x_ref, y_ref)):
+        total = jnp.zeros((PCS, LANES), F32)
+        squares = jnp.zeros((PCS, LANES), F32)
+        for first in range(0, in_ref.shape[1], LANES):
+            wide = in_ref[:, first : first + LANES].astype(F32)
+            total = total + wide
+            squares = squares + wide * wide
+        sq = jnp.sum(squares, 0, keepdims=True)
+        rest = jnp.broadcast_to(sq, (LANES - PCS, LANES))
+        line = jnp.sum(jnp.concatenate([total, rest], 0).T, 0, keepdims=True)
+        for peer in range(peers):
+            out_ref[peer, which : which + 1, :] = line
+
+
+def points_kernel(x_ref, y_ref, xa_ref, ya_ref):
+    width = 512
+    row = lax.broadcasted_iota(jnp.int32, (16, width), 0)
     for which, (in_ref, out_ref) in enumerate(((x_ref, xa_ref), (y_ref, ya_ref))):
-        total = jnp.zeros((1, PCS), F32)
-        total_sq = jnp.zeros((1, 1), F32)
-        for first in range(0, in_ref.shape[0], rows):
-            part = in_ref[first : first + rows, :]
-            wide = part.astype(F32)
-            sq = jnp.sum(wide * wide, 1, keepdims=True)
-            total = total + jnp.sum(wide, 0, keepdims=True)
-            total_sq = total_sq + jnp.sum(sq, 0, keepdims=True)
-            parts = split3(-0.5 * sq)
-            base = 3 * which
-            extra = jnp.where((lane >= 3 - base) & (lane < 6 - base), 1.0, 0.0)
+        base = 3 * which
+        for first in range(0, in_ref.shape[1], width):
+            wide = in_ref[:, first : first + width].astype(F32)
+            parts = split3(-0.5 * jnp.sum(wide * wide, 0, keepdims=True))
+            extra = jnp.where((row >= 3 - base) & (row < 6 - base), 1.0, 0.0)
             for k in range(3):
-                extra = jnp.where(lane == base + k, parts[k], extra)
-            out_ref[first : first + rows, 0:PCS] = part
-            out_ref[first : first + rows, PCS:LANES] = extra.astype(BF16)
-        for peer in range(peers):
-            stats_ref[peer, which : which + 1, 0:PCS] = total
-            stats_ref[peer, which : which + 1, PCS:LANES] = jnp.broadcast_to(
-                total_sq, (1, LANES - PCS)
-            )
+                extra = jnp.where(row == base + k, parts[k], extra)
+            pad = jnp.zeros((DEPTH - PCS - 16, width), F32)
+            whole = jnp.concatenate([wide, extra, pad], 0)
+            for part in range(0, width, LANES):
+                out_ref[first + part : first + part + LANES, :] = whole[
+                    :, part : part + LANES
+                ].T.astype(BF16)
 
 
 def gen_kernel(peers, weight_x, weight_y, xa_ref, ya_ref, stats_ref, scaling_ref, k_ref, out_ref):
@@ -65,7 +73,7 @@
     cross = jnp.where(lane < PCS, mean_x * mean_y, 0.0)
     mean_square = jnp.sum(square - 2.0 * cross, 1, keepdims=True) + offset_small
     factor = (2.0 * LOG2E) / (entropy_weight * mean_square)
-    block_cols, block_rows = 512, 256
+    block_cols, block_rows = 1024, 256
 
     def one_block(index, carry):
         first = pl.multiple_of(index * block_cols, block_cols)
@@ -90,7 +98,7 @@
                 out_ref[peer, pl.ds(index * (block_cols // LANES) + part // LANES, 1), :] = line
         return carry
 
-    lax.fori_loop(0, col_count // block_cols, one_block, 0)
+    lax.fori_loop(0, col_count // block_cols, one_block, 0, unroll=2)
 
 
 def spread(ref, values):
@@ -111,28 +119,26 @@
         for part in range(0, block, LANES):
             at = (first + part) // LANES
             line_ref[at : at + 1, :] = result[0:1, part : part + LANES]
-    whole = line_ref[...]
+    whole = line_ref[...].astype(out_ref.dtype)
     for peer in range(peers):
         out_ref[peer] = whole
 
 
-def col_kernel(peers, k_ref, sums_ref, mass_ref, out_ref, left_ref, line_ref):
-    spread(left_ref, mass_ref[...] / jnp.sum(sums_ref[...], 0))
-    count = k_ref.shape[0]
-    block = 512
-    for first in range(0, count, block):
-        result = lax.dot_general(
-            left_ref[...],
-            k_ref[first : first + block, :],
-            NT_DIMS,
-            preferred_element_type=F32,
-        )
+def col_kernel(peers, k_ref, sums_ref, mass_ref, out_ref, scaling_ref):
+    scaling = mass_ref[...] / jnp.sum(sums_ref[...].astype(F32), 0)
+    scaling_ref[...] = scaling.astype(BF16).astype(F32)
+    block = 256
+    for first in range(0, k_ref.shape[0], block):
+        acc = None
+        for t in range(scaling.shape[0]):
+            part = k_ref[first : first + block, t * LANES : (t + 1) * LANES].astype(F32)
+            term = part * scaling_ref[t : t + 1, :]
+            acc = term if acc is None else acc + term
         for part in range(0, block, LANES):
+            line = jnp.sum(acc[part : part + LANES, :].T, 0, keepdims=True)
             at = (first + part) // LANES
-            line_ref[at : at + 1, :] = result[0:1, part : part + LANES]
-    whole = line_ref[...]
-    for peer in range(peers):
-        out_ref[peer] = whole
+            for peer in range(peers):
+                out_ref[peer, at : at + 1, :] = line
 
 
 def fate_kernel(k_ref, sums_ref, mass_ref, labels_ref, out_ref, potential_ref, left_ref):
@@ -157,7 +163,7 @@
 def last_kernel(at_ref, sums_ref, mass_ref, fates_ref, potential_ref):
     sums = jnp.sum(sums_ref[...], 0)
     totals = jnp.sum(sums, 0, keepdims=True)
-    fates_ref[...] = (sums / totals).T
+    fates_ref[...] = sums / totals
     own = mass_ref[pl.ds(at_ref[0], 1), :]
     potential_ref[...] = entropy_weight * jnp.log(own / totals)
 
@@ -199,20 +205,27 @@
     scaling = source_scaling.reshape(lines_r, LANES)
     labels = labels.reshape(lines_c, LANES)
 
-    xa, ya, stats = call(
-        functools.partial(prep_kernel, col_size),
-        "prep",
-        (
-            shape((row_count, DEPTH), BF16),
-            shape((col_count, DEPTH), BF16),
-            shape((col_size, 2, LANES)),
-        ),
+    x_lines = pltpu.with_memory_space_constraint(source_pcs.T, pltpu.VMEM)
+    y_lines = pltpu.with_memory_space_constraint(target_pcs.T, pltpu.VMEM)
+    stats = call(
+        functools.partial(stats_kernel, col_size),
+        "stats",
+        shape((col_size, 2, LANES)),
         [VMEM] * 2,
-    )(source_pcs, target_pcs)
+    )(x_lines, y_lines)
     stats = lax.all_to_all(
         stats, ("row", "col"), 0, 0,
         axis_index_groups=diagonal_groups(row_size, col_size), tiled=True,
     )
+    xa, ya = call(
+        points_kernel,
+        "points",
+        (pltpu.VMEM((row_count, DEPTH), BF16), pltpu.VMEM((col_count, DEPTH), BF16)),
+        [VMEM] * 2,
+    )(x_lines, y_lines)
+    xa = pltpu.with_memory_space_constraint(xa, pltpu.VMEM)
+    ya = pltpu.with_memory_space_constraint(ya, pltpu.VMEM)
+    stats = pltpu.with_memory_space_constraint(stats, pltpu.VMEM)
     repeats = col_size // row_size
     k, sums = call(
         functools.partial(
@@ -231,12 +244,12 @@
     sums = call(
         functools.partial(row_kernel, col_size),
         "rows",
-        shape((col_size, lines_r, LANES)),
+        shape((col_size, lines_r, LANES), BF16),
         [VMEM] * 3,
         scratch,
     )(k, sums, target_mass)
     sums = lax.all_to_all(sums, "col", 0, 0, tiled=True)
-    scratch = [pltpu.VMEM((16, row_count), BF16), pltpu.VMEM((lines_c, LANES), F32)]
+    scratch = [pltpu.VMEM((lines_r, LANES), F32)]
     sums = call(
         functools.partial(col_kernel, row_size),
         "cols",
@@ -257,10 +270,10 @@
     fates, source_potential = call(
         last_kernel,
         "last",
-        (shape((LANES, SETS)), shape((1, LANES))),
+        (shape((SETS, LANES)), shape((1, LANES))),
         [SMEM, VMEM, VMEM],
     )(at, sums, source_mass)
-    return fates, source_potential.reshape(LANES), target_potential.reshape(col_count)
+    return fates.T, source_potential.reshape(LANES), target_potential.reshape(col_count)
 
 
 def solution(mesh):

time: 138 us -> 122 us (0.88)
  blocking collectives: 66.6 us -> 37.8 us
  starting transfers between devices: 4.39 us -> 17.9 us
  waiting for transfers between devices: 15.5 us -> 23.8 us
  Pallas kernels: 42.9 us -> 36.8 us
  local copies, waits for them, and re-layouts: 5.71 us -> 4.16 us
    all_to_all x1 -> x0, blocking collectives: 24.1 us -> none  [on_device(): lax.all_to_all(stats, ('row', 'col'), 0, 0, axis_index_groups=diagonal_gr...]
    all_to_all x0 -> x1, starting transfers between devices: none -> 14 us  [on_device(): lax.all_to_all(stats, ('row', 'col'), 0, 0, axis_index_groups=diagonal_gr...]
    all_to_all x0 -> x1, waiting for transfers between devices: none -> 7.52 us  [on_device(): lax.all_to_all(stats, ('row', 'col'), 0, 0, axis_index_groups=diagonal_gr...]
    all_to_all x1, blocking collectives: 20.9 us -> 16 us  [on_device(): sums = lax.all_to_all(sums, 'col', 0, 0, tiled=True)]
    pallas_call x1, Pallas kernels: 14.9 us -> 12.5 us  [on_device(): call(functools.partial(gen_kernel, row_size, 1.0 / (repeats * row_count *...]
    pallas_call x1, Pallas kernels: 10.5 us -> 8.22 us  [on_device(): call(functools.partial(col_kernel, row_size), 'cols', shape((row_size, li...]
    unnamed x9 -> x10, local copies, waits for them, and re-layouts: 5.71 us -> 4.16 us
    pallas_call x2 -> x3, Pallas kernels: 3.75 us -> 2.32 us  [the longest x1 0.99 us: on_device(): call(functools.partial(stats_kernel, col_size), 'stats', shape((col_size,...]
  transfers between devices with their start and end apart: 1 -> 2, of which waited for: 1 -> 2; matrix products, arithmetic and copies ran while one was open for 0% -> 0% of each run, Pallas kernels for 0% -> 1%
where the time goes in v2:
time: 122 us; the launch traced here: 121 us
  blocking collectives  37.8 us (31%)
  Pallas kernels  36.8 us (30%)
  waiting for transfers between devices  23.8 us (20%)
  starting transfers between devices  17.9 us (15%)
  local copies, waits for them, and re-layouts  4.16 us (3%)
    all_to_all x2, blocking collectives, on_device(): sums = lax.all_to_all(sums, 'row', 0, 0, tiled=True)  21.9 us
    all_to_all x1, waiting for transfers between devices, on_device(): sums = lax.all_to_all(sums, 'col', 0, 0, tiled=True)  16.3 us
    all_to_all x1, blocking collectives, on_device(): sums = lax.all_to_all(sums, 'col', 0, 0, tiled=True)  16 us
    all_to_all x1, starting transfers between devices, on_device(): lax.all_to_all(stats, ('row', 'col'), 0, 0, axis_index_groups=diagonal_gr...  14 us
    pallas_call x1, Pallas kernels, on_device(): call(functools.partial(gen_kernel, row_size, 1.0 / (repeats * row_count *...  12.5 us
    pallas_call x1, Pallas kernels, on_device(): call(functools.partial(col_kernel, row_size), 'cols', shape((row_size, li...  8.22 us
    pallas_call x1, Pallas kernels, on_device(): call(fate_kernel, 'fate', (shape((lines_r, SETS, LANES)), shape((lines_c,...  7.66 us
    all_to_all x1, waiting for transfers between devices, on_device(): lax.all_to_all(stats, ('row', 'col'), 0, 0, axis_index_groups=diagonal_gr...  7.52 us
  transfers between devices with their start and end apart: 2, of which 2 were waited for; matrix products, arithmetic and copies ran while one was open for 0% of the time, Pallas kernels for 1%

profile of v2, /device:TPU:1, one launch (start us, length us, event | category | flops | bytes accessed | tf_op | source)
XLA Modules:
  0.0 121.1 jit_solution(16243712585092233246)
XLA Ops:
  0.6 0.0 copy-start
  0.6 1.0 copy-done
  1.7 0.0 copy-start.2
  1.7 1.0 copy-done.2
  2.7 1.0 stats.1
  3.7 14.0 %all-to-all-start = ((f32[32,2,128]{2,1,0:T(2,128)}), f32[32,2,128]{2,1,0:T(2,128)S(1)}, u32[]{:S(2)}, u32[]{:S(2)}) async-start(f32[32,2,128]{2,1,0:T(2,128)} %stats.1), calls=%async_computation | async-start | bytes 65536 | tf_op jit(solution)/shard_map/all_to_all | solution.py:216
  17.7 0.0 copy-start.1
  17.7 1.0 copy-done.1
  18.7 0.0 copy-start.3
  18.7 1.0 copy-done.3
  19.8 0.7 points.1
  20.5 7.5 %all-to-all-done.stats_ref = f32[32,2,128]{2,1,0:T(2,128)S(1)} async-done(((f32[32,2,128]{2,1,0:T(2,128)}), f32[32,2,128]{2,1,0:T(2,128)S(1)}, u32[]{:S(2)}, u32[]{:S(2)}) %all-to-all-start) | async-done | bytes 32800 | tf_op jit(solution)/shard_map/all_to_all | solution.py:216
  28.0 12.5 %gen.1 = (bf16[4096,4096]{1,0:T(8,128)(2,1)S(1)}, f32[8,32,128]{2,1,0:T(8,128)}) custom-call(bf16[4096,128]{1,0:T(8,128)(2,1)S(1)} %get-tuple-element.11.xa_ref, bf16[4096,128]{1,0:T(8,128)(2,1)S(1)} %get-tuple-element.12.ya_ref, f32[32,2,128]{2,1,0:T(2,128)S(1)} %all-to-all-done.stats_ref, f32[32,128]{1,0:T(8,128)} %bitcast.19), custom_call_target="tpu_custom_call" | custom-call | tf_op jit(solution)/shard_map/gen/pallas_call | solution.py:230
  40.5 10.0 %all_to_all.25.sums_ref = f32[8,32,128]{2,1,0:T(8,128)} all-to-all(f32[8,32,128]{2,1,0:T(8,128)} %get-tuple-element.14), channel_id=1, replica_groups=mesh['row'=8,'col'=32] {'row'}, dimensions={0} | all-to-all | bytes 262144 | tf_op jit(solution)/shard_map/all_to_all | solution.py:242
  50.5 6.1 %rows.1 = bf16[32,32,128]{2,1,0:T(8,128)(2,1)} custom-call(bf16[4096,4096]{1,0:T(8,128)(2,1)S(1)} %get-tuple-element.13.k_ref, f32[8,32,128]{2,1,0:T(8,128)} %all_to_all.25.sums_ref, f32[32,128]{1,0:T(8,128)} %bitcast.16), custom_call_target="tpu_custom_call" | custom-call | tf_op jit(solution)/shard_map/rows/pallas_call | solution.py:244
  56.6 16.0 %all_to_all.26.sums_ref = bf16[32,32,128]{2,1,0:T(8,128)(2,1)} all-to-all(bf16[32,32,128]{2,1,0:T(8,128)(2,1)} %rows.1), channel_id=1, replica_groups=mesh['row'=8,'col'=32] {'col'}, dimensions={0} | all-to-all | bytes 524288 | tf_op jit(solution)/shard_map/all_to_all | solution.py:251
  72.5 0.0 copy-start.4
  72.5 8.2 %cols.1 = f32[8,32,128]{2,1,0:T(8,128)} custom-call(bf16[4096,4096]{1,0:T(8,128)(2,1)S(1)} %get-tuple-element.13.k_ref, bf16[32,32,128]{2,1,0:T(8,128)(2,1)} %all_to_all.26.sums_ref, f32[32,128]{1,0:T(8,128)} %bitcast.14), custom_call_target="tpu_custom_call" | custom-call | tf_op jit(solution)/shard_map/cols/pallas_call | solution.py:253
  80.8 11.9 %all_to_all.27.sums_ref = f32[8,32,128]{2,1,0:T(8,128)} all-to-all(f32[8,32,128]{2,1,0:T(8,128)} %cols.1), channel_id=1, replica_groups=mesh['row'=8,'col'=32] {'row'}, dimensions={0} | all-to-all | bytes 262144 | tf_op jit(solution)/shard_map/all_to_all | solution.py:260
  92.6 7.7 %fate.1 = (f32[32,32,128]{2,1,0:T(8,128)}, f32[32,128]{1,0:T(8,128)}) custom-call(bf16[4096,4096]{1,0:T(8,128)(2,1)S(1)} %get-tuple-element.13.k_ref, f32[8,32,128]{2,1,0:T(8,128)} %all_to_all.27.sums_ref, f32[32,128]{1,0:T(8,128)} %bitcast.17, s32[32,128]{1,0:T(8,128)} %bitcast.18), custom_call_target="tpu_custom_call" | custom-call | tf_op jit(solution)/shard_map/fate/pallas_call | solution.py:261
  100.3 3.9 %all-to-all-start.4 = ((f32[32,32,128]{2,1,0:T(8,128)}), f32[32,32,128]{2,1,0:T(8,128)S(1)}, u32[]{:S(2)}, u32[]{:S(2)}) async-start(f32[32,32,128]{2,1,0:T(8,128)} %get-tuple-element.15), calls=%async_computation.4 | async-start | bytes 1048576 | tf_op jit(solution)/shard_map/all_to_all | solution.py:268
  104.2 16.3 %all-to-all-done.4.sums_ref = f32[32,32,128]{2,1,0:T(8,128)S(1)} async-done(((f32[32,32,128]{2,1,0:T(8,128)}), f32[32,32,128]{2,1,0:T(8,128)S(1)}, u32[]{:S(2)}, u32[]{:S(2)}) %all-to-all-start.4) | async-done | bytes 524320 | tf_op jit(solution)/shard_map/all_to_all | solution.py:268
  120.5 0.0 copy-done.4
  120.5 0.7 last.1
Async XLA Ops:
  0.6 1.0 copy-start
  1.7 1.0 copy-start.2
  3.7 24.3 %all-to-all-start = ((f32[32,2,128]{2,1,0:T(2,128)}), f32[32,2,128]{2,1,0:T(2,128)S(1)}, u32[]{:S(2)}, u32[]{:S(2)}) async-start(f32[32,2,128]{2,1,0:T(2,128)} %stats.1), calls=%async_computation | async-start | bytes 65536 | tf_op jit(solution)/shard_map/all_to_all | solution.py:216
  17.7 1.0 copy-start.1
  18.7 1.0 copy-start.3
  72.5 48.0 %copy-start.4 = (f32[4096]{0:T(1024)S(1)}, f32[4096]{0:T(1024)}, u32[]{:S(2)}) copy-start(f32[4096]{0:T(1024)} %param.8) | copy-start | bytes 49156
  100.3 20.2 %all-to-all-start.4 = ((f32[32,32,128]{2,1,0:T(8,128)}), f32[32,32,128]{2,1,0:T(8,128)S(1)}, u32[]{:S(2)}, u32[]{:S(2)}) async-start(f32[32,32,128]{2,1,0:T(8,128)} %get-tuple-element.15), calls=%async_computation.4 | async-start | bytes 1048576 | tf_op jit(solution)/shard_map/all_to_all | solution.py:268

commit v3 on v2

--- a/solution.py
+++ b/solution.py
@@ -12,6 +12,8 @@
 PCS = 64
 LANES = 128
 DEPTH = 128
+WIRE_ROWS = 40
+LEAST_POWER = -111.0
 entropy_weight = 0.5
 offset_small = 1e-06
 LOG2E = 1.4426950408889634
@@ -29,8 +31,15 @@
     return hi, mid, lo
 
 
-def stats_kernel(peers, x_ref, y_ref, out_ref):
+def stats_kernel(peers, x_hbm, y_hbm, out_ref, x_ref, y_ref, sems):
+    copies = [
+        pltpu.make_async_copy(x_hbm, x_ref, sems.at[0]),
+        pltpu.make_async_copy(y_hbm, y_ref, sems.at[1]),
+    ]
+    for copy in copies:
+        copy.start()
     for which, in_ref in enumerate((x_ref, y_ref)):
+        copies[which].wait()
         total = jnp.zeros((PCS, LANES), F32)
         squares = jnp.zeros((PCS, LANES), F32)
         for first in range(0, in_ref.shape[1], LANES):
@@ -157,11 +166,20 @@
             left_ref[...], k_ref[:, first : first + block], preferred_element_type=F32
         )
         for part in range(0, block, LANES):
-            out_ref[(first + part) // LANES] = result[:, part : part + LANES]
+            share = result[:, part : part + LANES]
+            top = jnp.log2(jnp.max(share, 0, keepdims=True))
+            power = jnp.clip(jnp.floor(top) + 1.0, LEAST_POWER, 127.0)
+            scaled = jnp.minimum(share * jnp.exp2(15.0 - power) + 0.5, 32767.0)
+            rest = jnp.broadcast_to(power, (WIRE_ROWS - SETS, LANES))
+            coded = jnp.concatenate([scaled, rest], 0).astype(jnp.int32)
+            out_ref[(first + part) // LANES] = coded.astype(jnp.int16)
 
 
 def last_kernel(at_ref, sums_ref, mass_ref, fates_ref, potential_ref):
-    sums = jnp.sum(sums_ref[...], 0)
+    sums = jnp.zeros((SETS, LANES), F32)
+    for peer in range(sums_ref.shape[0]):
+        coded = sums_ref[peer].astype(jnp.int32).astype(F32)
+        sums = sums + coded[0:SETS, :] * jnp.exp2(coded[SETS : SETS + 1, :] - 15.0)
     totals = jnp.sum(sums, 0, keepdims=True)
     fates_ref[...] = sums / totals
     own = mass_ref[pl.ds(at_ref[0], 1), :]
@@ -205,13 +223,17 @@
     scaling = source_scaling.reshape(lines_r, LANES)
     labels = labels.reshape(lines_c, LANES)
 
-    x_lines = pltpu.with_memory_space_constraint(source_pcs.T, pltpu.VMEM)
-    y_lines = pltpu.with_memory_space_constraint(target_pcs.T, pltpu.VMEM)
+    x_lines, y_lines = source_pcs.T, target_pcs.T
     stats = call(
         functools.partial(stats_kernel, col_size),
         "stats",
         shape((col_size, 2, LANES)),
-        [VMEM] * 2,
+        [pl.BlockSpec(memory_space=pltpu.HBM)] * 2,
+        [
+            pltpu.VMEM(x_lines.shape, BF16),
+            pltpu.VMEM(y_lines.shape, BF16),
+            pltpu.SemaphoreType.DMA((2,)),
+        ],
     )(x_lines, y_lines)
     stats = lax.all_to_all(
         stats, ("row", "col"), 0, 0,
@@ -261,7 +283,7 @@
     sums, target_potential = call(
         fate_kernel,
         "fate",
-        (shape((lines_r, SETS, LANES)), shape((lines_c, LANES))),
+        (shape((lines_r, WIRE_ROWS, LANES), jnp.int16), shape((lines_c, LANES))),
         [VMEM] * 4,
         [pltpu.VMEM((SETS, col_count), BF16)],
     )(k, sums, target_mass, labels)

time: 122 us -> 119 us (0.975)
  waiting for transfers between devices: 23.8 us -> 20.4 us
    all_to_all x1, waiting for transfers between devices: 16.3 us -> 12.8 us  [on_device(): sums = lax.all_to_all(sums, 'col', 0, 0, tiled=True)]
where the time goes in v3:
time: 119 us; the launch traced here: 118 us
  blocking collectives  37.8 us (32%)
  Pallas kernels  37 us (31%)
  waiting for transfers between devices  20.4 us (17%)
  starting transfers between devices  17.9 us (15%)
  local copies, waits for them, and re-layouts  4.16 us (3%)
    all_to_all x2, blocking collectives, on_device(): sums = lax.all_to_all(sums, 'row', 0, 0, tiled=True)  21.9 us
    all_to_all x1, blocking collectives, on_device(): sums = lax.all_to_all(sums, 'col', 0, 0, tiled=True)  16 us
    all_to_all x1, starting transfers between devices, on_device(): lax.all_to_all(stats, ('row', 'col'), 0, 0, axis_index_groups=diagonal_gr...  14 us
    all_to_all x1, waiting for transfers between devices, on_device(): sums = lax.all_to_all(sums, 'col', 0, 0, tiled=True)  12.8 us
    pallas_call x1, Pallas kernels, on_device(): call(functools.partial(gen_kernel, row_size, 1.0 / (repeats * row_count *...  12.5 us
    pallas_call x1, Pallas kernels, on_device(): call(functools.partial(col_kernel, row_size), 'cols', shape((row_size, li...  8.22 us
    pallas_call x1, Pallas kernels, on_device(): call(fate_kernel, 'fate', (shape((lines_r, WIRE_ROWS, LANES), jnp.int16),...  7.59 us
    all_to_all x1, waiting for transfers between devices, on_device(): lax.all_to_all(stats, ('row', 'col'), 0, 0, axis_index_groups=diagonal_gr...  7.52 us
  transfers between devices with their start and end apart: 2, of which 2 were waited for; matrix products, arithmetic and copies ran while one was open for 0% of the time, Pallas kernels for 1%

profile of v3, /device:TPU:1, one launch (start us, length us, event | category | flops | bytes accessed | tf_op | source)
XLA Modules:
  0.0 117.9 jit_solution(3935390541574899767)
XLA Ops:
  0.6 0.0 copy-start
  0.6 1.0 copy-done
  1.7 0.0 copy-start.2
  1.7 1.0 copy-done.2
  2.7 1.2 %stats.1 = f32[32,2,128]{2,1,0:T(2,128)} custom-call(bf16[64,4096]{1,0:T(8,128)(2,1)S(1)} %bitcast.10, bf16[64,4096]{1,0:T(8,128)(2,1)S(1)} %bitcast.12), custom_call_target="tpu_custom_call" | custom-call | tf_op jit(solution)/shard_map/stats/pallas_call | solution.py:227
  3.9 14.0 %all-to-all-start = ((f32[32,2,128]{2,1,0:T(2,128)}), f32[32,2,128]{2,1,0:T(2,128)S(1)}, u32[]{:S(2)}, u32[]{:S(2)}) async-start(f32[32,2,128]{2,1,0:T(2,128)} %stats.1), calls=%async_computation | async-start | bytes 65536 | tf_op jit(solution)/shard_map/all_to_all | solution.py:238
  17.9 0.0 copy-start.1
  17.9 1.0 copy-done.1
  19.0 0.0 copy-start.3
  19.0 1.0 copy-done.3
  20.0 0.7 points.1
  20.7 7.5 %all-to-all-done.stats_ref = f32[32,2,128]{2,1,0:T(2,128)S(1)} async-done(((f32[32,2,128]{2,1,0:T(2,128)}), f32[32,2,128]{2,1,0:T(2,128)S(1)}, u32[]{:S(2)}, u32[]{:S(2)}) %all-to-all-start) | async-done | bytes 32800 | tf_op jit(solution)/shard_map/all_to_all | solution.py:238
  28.2 12.5 %gen.1 = (bf16[4096,4096]{1,0:T(8,128)(2,1)S(1)}, f32[8,32,128]{2,1,0:T(8,128)}) custom-call(bf16[4096,128]{1,0:T(8,128)(2,1)S(1)} %get-tuple-element.11.xa_ref, bf16[4096,128]{1,0:T(8,128)(2,1)S(1)} %get-tuple-element.12.ya_ref, f32[32,2,128]{2,1,0:T(2,128)S(1)} %all-to-all-done.stats_ref, f32[32,128]{1,0:T(8,128)} %bitcast.19), custom_call_target="tpu_custom_call" | custom-call | tf_op jit(solution)/shard_map/gen/pallas_call | solution.py:252
  40.7 10.0 %all_to_all.25.sums_ref = f32[8,32,128]{2,1,0:T(8,128)} all-to-all(f32[8,32,128]{2,1,0:T(8,128)} %get-tuple-element.14), channel_id=1, replica_groups=mesh['row'=8,'col'=32] {'row'}, dimensions={0} | all-to-all | bytes 262144 | tf_op jit(solution)/shard_map/all_to_all | solution.py:264
  50.7 6.1 %rows.1 = bf16[32,32,128]{2,1,0:T(8,128)(2,1)} custom-call(bf16[4096,4096]{1,0:T(8,128)(2,1)S(1)} %get-tuple-element.13.k_ref, f32[8,32,128]{2,1,0:T(8,128)} %all_to_all.25.sums_ref, f32[32,128]{1,0:T(8,128)} %bitcast.16), custom_call_target="tpu_custom_call" | custom-call | tf_op jit(solution)/shard_map/rows/pallas_call | solution.py:266
  56.8 16.0 %all_to_all.26.sums_ref = bf16[32,32,128]{2,1,0:T(8,128)(2,1)} all-to-all(bf16[32,32,128]{2,1,0:T(8,128)(2,1)} %rows.1), channel_id=1, replica_groups=mesh['row'=8,'col'=32] {'col'}, dimensions={0} | all-to-all | bytes 524288 | tf_op jit(solution)/shard_map/all_to_all | solution.py:273
  72.8 0.0 copy-start.4
  72.8 8.2 %cols.1 = f32[8,32,128]{2,1,0:T(8,128)} custom-call(bf16[4096,4096]{1,0:T(8,128)(2,1)S(1)} %get-tuple-element.13.k_ref, bf16[32,32,128]{2,1,0:T(8,128)(2,1)} %all_to_all.26.sums_ref, f32[32,128]{1,0:T(8,128)} %bitcast.14), custom_call_target="tpu_custom_call" | custom-call | tf_op jit(solution)/shard_map/cols/pallas_call | solution.py:275
  81.0 11.9 %all_to_all.27.sums_ref = f32[8,32,128]{2,1,0:T(8,128)} all-to-all(f32[8,32,128]{2,1,0:T(8,128)} %cols.1), channel_id=1, replica_groups=mesh['row'=8,'col'=32] {'row'}, dimensions={0} | all-to-all | bytes 262144 | tf_op jit(solution)/shard_map/all_to_all | solution.py:282
  92.9 7.6 %fate.1 = (s16[32,40,128]{2,1,0:T(8,128)(2,1)}, f32[32,128]{1,0:T(8,128)}) custom-call(bf16[4096,4096]{1,0:T(8,128)(2,1)S(1)} %get-tuple-element.13.k_ref, f32[8,32,128]{2,1,0:T(8,128)} %all_to_all.27.sums_ref, f32[32,128]{1,0:T(8,128)} %bitcast.17, s32[32,128]{1,0:T(8,128)} %bitcast.18), custom_call_target="tpu_custom_call" | custom-call | tf_op jit(solution)/shard_map/fate/pallas_call | solution.py:283
  100.4 3.9 %all-to-all-start.4 = ((s16[32,40,128]{2,1,0:T(8,128)(2,1)}), s16[32,40,128]{2,1,0:T(8,128)(2,1)S(1)}, u32[]{:S(2)}, u32[]{:S(2)}) async-start(s16[32,40,128]{2,1,0:T(8,128)(2,1)} %get-tuple-element.15), calls=%async_computation.4 | async-start | bytes 655360 | tf_op jit(solution)/shard_map/all_to_all | solution.py:290
  104.3 12.8 %all-to-all-done.4.sums_ref = s16[32,40,128]{2,1,0:T(8,128)(2,1)S(1)} async-done(((s16[32,40,128]{2,1,0:T(8,128)(2,1)}), s16[32,40,128]{2,1,0:T(8,128)(2,1)S(1)}, u32[]{:S(2)}, u32[]{:S(2)}) %all-to-all-start.4) | async-done | bytes 327712 | tf_op jit(solution)/shard_map/all_to_all | solution.py:290
  117.2 0.0 copy-done.4
  117.2 0.7 last.1
Async XLA Ops:
  0.6 1.0 copy-start
  1.7 1.0 copy-start.2
  3.9 24.3 %all-to-all-start = ((f32[32,2,128]{2,1,0:T(2,128)}), f32[32,2,128]{2,1,0:T(2,128)S(1)}, u32[]{:S(2)}, u32[]{:S(2)}) async-start(f32[32,2,128]{2,1,0:T(2,128)} %stats.1), calls=%async_computation | async-start | bytes 65536 | tf_op jit(solution)/shard_map/all_to_all | solution.py:238
  17.9 1.0 copy-start.1
  19.0 1.0 copy-start.3
  72.8 44.4 %copy-start.4 = (f32[4096]{0:T(1024)S(1)}, f32[4096]{0:T(1024)}, u32[]{:S(2)}) copy-start(f32[4096]{0:T(1024)} %param.8) | copy-start | bytes 49156
  100.4 16.7 %all-to-all-start.4 = ((s16[32,40,128]{2,1,0:T(8,128)(2,1)}), s16[32,40,128]{2,1,0:T(8,128)(2,1)S(1)}, u32[]{:S(2)}, u32[]{:S(2)}) async-start(s16[32,40,128]{2,1,0:T(8,128)(2,1)} %get-tuple-element.15), calls=%async_computation.4 | async-start | bytes 655360 | tf_op jit(solution)/shard_map/all_to_all | solution.py:290

commit v4 on v3

--- a/solution.py
+++ b/solution.py
@@ -72,7 +72,7 @@
                 ].T.astype(BF16)
 
 
-def gen_kernel(peers, weight_x, weight_y, xa_ref, ya_ref, stats_ref, scaling_ref, k_ref, out_ref):
+def gen_kernel(peers, weight_x, weight_y, xa_ref, ya_ref, stats_ref, scaling_ref, k_ref, out_ref, line_ref):
     row_count, col_count = xa_ref.shape[0], ya_ref.shape[0]
     sums = jnp.sum(stats_ref[...], 0)
     mean_x = sums[0:1, :] * weight_x
@@ -82,7 +82,7 @@
     cross = jnp.where(lane < PCS, mean_x * mean_y, 0.0)
     mean_square = jnp.sum(square - 2.0 * cross, 1, keepdims=True) + offset_small
     factor = (2.0 * LOG2E) / (entropy_weight * mean_square)
-    block_cols, block_rows = 1024, 256
+    block_cols, block_rows = 2048, 256
 
     def one_block(index, carry):
         first = pl.multiple_of(index * block_cols, block_cols)
@@ -103,11 +103,13 @@
                 acc = term if acc is None else acc + term
         for part in range(0, block_cols, LANES):
             line = jnp.sum(acc[part : part + LANES, :].T, 0, keepdims=True)
-            for peer in range(peers):
-                out_ref[peer, pl.ds(index * (block_cols // LANES) + part // LANES, 1), :] = line
+            line_ref[pl.ds(index * (block_cols // LANES) + part // LANES, 1), :] = line
         return carry
 
     lax.fori_loop(0, col_count // block_cols, one_block, 0, unroll=2)
+    whole = line_ref[...].astype(out_ref.dtype)
+    for peer in range(peers):
+        out_ref[peer] = whole
 
 
 def spread(ref, values):
@@ -118,7 +120,7 @@
 
 
 def row_kernel(peers, k_ref, sums_ref, mass_ref, out_ref, left_ref, line_ref):
-    spread(left_ref, mass_ref[...] / jnp.sum(sums_ref[...], 0))
+    spread(left_ref, mass_ref[...] / jnp.sum(sums_ref[...].astype(F32), 0))
     count = k_ref.shape[1]
     block = 512
     for first in range(0, count, block):
@@ -224,6 +226,8 @@
     labels = labels.reshape(lines_c, LANES)
 
     x_lines, y_lines = source_pcs.T, target_pcs.T
+    x_far = pltpu.with_memory_space_constraint(x_lines, pltpu.HBM)
+    y_far = pltpu.with_memory_space_constraint(y_lines, pltpu.HBM)
     stats = call(
         functools.partial(stats_kernel, col_size),
         "stats",
@@ -234,7 +238,7 @@
             pltpu.VMEM(y_lines.shape, BF16),
             pltpu.SemaphoreType.DMA((2,)),
         ],
-    )(x_lines, y_lines)
+    )(x_far, y_far)
     stats = lax.all_to_all(
         stats, ("row", "col"), 0, 0,
         axis_index_groups=diagonal_groups(row_size, col_size), tiled=True,
@@ -257,8 +261,9 @@
             1.0 / (col_count * col_size),
         ),
         "gen",
-        (pltpu.VMEM((col_count, row_count), BF16), shape((row_size, lines_c, LANES))),
+        (pltpu.VMEM((col_count, row_count), BF16), shape((row_size, lines_c, LANES), BF16)),
         [VMEM] * 4,
+        [pltpu.VMEM((lines_c, LANES), F32)],
     )(xa, ya, stats, scaling)
     k = pltpu.with_memory_space_constraint(k, pltpu.VMEM)
     sums = lax.all_to_all(sums, "row", 0, 0, tiled=True)

time: 119 us -> 117 us (0.983)
  local copies, waits for them, and re-layouts: 4.16 us -> 2.08 us
    unnamed x10 -> x6, local copies, waits for them, and re-layouts: 4.16 us -> 2.08 us
where the time goes in v4:
time: 117 us; the launch traced here: 116 us
  Pallas kernels  37.5 us (32%)
  blocking collectives  37.4 us (32%)
  waiting for transfers between devices  20.4 us (17%)
  starting transfers between devices  17.9 us (15%)
  local copies, waits for them, and re-layouts  2.08 us (2%)
    all_to_all x2, blocking collectives, on_device(): sums = lax.all_to_all(sums, 'row', 0, 0, tiled=True)  21.4 us
    all_to_all x1, blocking collectives, on_device(): sums = lax.all_to_all(sums, 'col', 0, 0, tiled=True)  16 us
    all_to_all x1, starting transfers between devices, on_device(): lax.all_to_all(stats, ('row', 'col'), 0, 0, axis_index_groups=diagonal_gr...  14 us
    all_to_all x1, waiting for transfers between devices, on_device(): sums = lax.all_to_all(sums, 'col', 0, 0, tiled=True)  12.8 us
    pallas_call x1, Pallas kernels, on_device(): call(functools.partial(gen_kernel, row_size, 1.0 / (repeats * row_count *...  12.1 us
    pallas_call x1, Pallas kernels, on_device(): call(functools.partial(col_kernel, row_size), 'cols', shape((row_size, li...  8.21 us
    pallas_call x1, Pallas kernels, on_device(): call(fate_kernel, 'fate', (shape((lines_r, WIRE_ROWS, LANES), jnp.int16),...  7.6 us
    all_to_all x1, waiting for transfers between devices, on_device(): lax.all_to_all(stats, ('row', 'col'), 0, 0, axis_index_groups=diagonal_gr...  7.52 us
  transfers between devices with their start and end apart: 2, of which 2 were waited for; matrix products, arithmetic and copies ran while one was open for 0% of the time, Pallas kernels for 1%

profile of v4, /device:TPU:1, one launch (start us, length us, event | category | flops | bytes accessed | tf_op | source)
XLA Modules:
  0.0 115.9 jit_solution(13156656777117342731)
XLA Ops:
  0.6 2.2 %stats.1 = f32[32,2,128]{2,1,0:T(2,128)} custom-call(bf16[64,4096]{1,0:T(8,128)(2,1)} %bitcast.10, bf16[64,4096]{1,0:T(8,128)(2,1)} %bitcast.12), custom_call_target="tpu_custom_call" | custom-call | tf_op jit(solution)/shard_map/stats/pallas_call | solution.py:231
  2.8 14.0 %all-to-all-start = ((f32[32,2,128]{2,1,0:T(2,128)}), f32[32,2,128]{2,1,0:T(2,128)S(1)}, u32[]{:S(2)}, u32[]{:S(2)}) async-start(f32[32,2,128]{2,1,0:T(2,128)} %stats.1), calls=%async_computation | async-start | bytes 65536 | tf_op jit(solution)/shard_map/all_to_all | solution.py:242
  16.8 0.0 copy-start
  16.8 1.0 copy-done
  17.8 0.0 copy-start.1
  17.8 1.0 copy-done.1
  18.9 0.7 points.1
  19.6 7.5 %all-to-all-done.stats_ref = f32[32,2,128]{2,1,0:T(2,128)S(1)} async-done(((f32[32,2,128]{2,1,0:T(2,128)}), f32[32,2,128]{2,1,0:T(2,128)S(1)}, u32[]{:S(2)}, u32[]{:S(2)}) %all-to-all-start) | async-done | bytes 32800 | tf_op jit(solution)/shard_map/all_to_all | solution.py:242
  27.1 12.1 %gen.1 = (bf16[4096,4096]{1,0:T(8,128)(2,1)S(1)}, bf16[8,32,128]{2,1,0:T(8,128)(2,1)}) custom-call(bf16[4096,128]{1,0:T(8,128)(2,1)S(1)} %get-tuple-element.11.xa_ref, bf16[4096,128]{1,0:T(8,128)(2,1)S(1)} %get-tuple-element.12.ya_ref, f32[32,2,128]{2,1,0:T(2,128)S(1)} %all-to-all-done.stats_ref, f32[32,128]{1,0:T(8,128)} %bitcast.19), custom_call_target="tpu_custom_call" | custom-call | tf_op jit(solution)/shard_map/gen/pallas_call | solution.py:256
  39.2 9.6 %all_to_all.25.sums_ref = bf16[8,32,128]{2,1,0:T(8,128)(2,1)} all-to-all(bf16[8,32,128]{2,1,0:T(8,128)(2,1)} %get-tuple-element.14), channel_id=1, replica_groups=mesh['row'=8,'col'=32] {'row'}, dimensions={0} | all-to-all | bytes 131072 | tf_op jit(solution)/shard_map/all_to_all | solution.py:269
  48.8 6.0 %rows.1 = bf16[32,32,128]{2,1,0:T(8,128)(2,1)} custom-call(bf16[4096,4096]{1,0:T(8,128)(2,1)S(1)} %get-tuple-element.13.k_ref, bf16[8,32,128]{2,1,0:T(8,128)(2,1)} %all_to_all.25.sums_ref, f32[32,128]{1,0:T(8,128)} %bitcast.16), custom_call_target="tpu_custom_call" | custom-call | tf_op jit(solution)/shard_map/rows/pallas_call | solution.py:271
  54.8 16.0 %all_to_all.26.sums_ref = bf16[32,32,128]{2,1,0:T(8,128)(2,1)} all-to-all(bf16[32,32,128]{2,1,0:T(8,128)(2,1)} %rows.1), channel_id=1, replica_groups=mesh['row'=8,'col'=32] {'col'}, dimensions={0} | all-to-all | bytes 524288 | tf_op jit(solution)/shard_map/all_to_all | solution.py:278
  70.8 0.0 copy-start.2
  70.8 8.2 %cols.1 = f32[8,32,128]{2,1,0:T(8,128)} custom-call(bf16[4096,4096]{1,0:T(8,128)(2,1)S(1)} %get-tuple-element.13.k_ref, bf16[32,32,128]{2,1,0:T(8,128)(2,1)} %all_to_all.26.sums_ref, f32[32,128]{1,0:T(8,128)} %bitcast.14), custom_call_target="tpu_custom_call" | custom-call | tf_op jit(solution)/shard_map/cols/pallas_call | solution.py:280
  79.0 11.8 %all_to_all.27.sums_ref = f32[8,32,128]{2,1,0:T(8,128)} all-to-all(f32[8,32,128]{2,1,0:T(8,128)} %cols.1), channel_id=1, replica_groups=mesh['row'=8,'col'=32] {'row'}, dimensions={0} | all-to-all | bytes 262144 | tf_op jit(solution)/shard_map/all_to_all | solution.py:287
  90.9 7.6 %fate.1 = (s16[32,40,128]{2,1,0:T(8,128)(2,1)}, f32[32,128]{1,0:T(8,128)}) custom-call(bf16[4096,4096]{1,0:T(8,128)(2,1)S(1)} %get-tuple-element.13.k_ref, f32[8,32,128]{2,1,0:T(8,128)} %all_to_all.27.sums_ref, f32[32,128]{1,0:T(8,128)} %bitcast.17, s32[32,128]{1,0:T(8,128)} %bitcast.18), custom_call_target="tpu_custom_call" | custom-call | tf_op jit(solution)/shard_map/fate/pallas_call | solution.py:288
  98.4 3.9 %all-to-all-start.4 = ((s16[32,40,128]{2,1,0:T(8,128)(2,1)}), s16[32,40,128]{2,1,0:T(8,128)(2,1)S(1)}, u32[]{:S(2)}, u32[]{:S(2)}) async-start(s16[32,40,128]{2,1,0:T(8,128)(2,1)} %get-tuple-element.15), calls=%async_computation.4 | async-start | bytes 655360 | tf_op jit(solution)/shard_map/all_to_all | solution.py:295
  102.3 12.8 %all-to-all-done.4.sums_ref = s16[32,40,128]{2,1,0:T(8,128)(2,1)S(1)} async-done(((s16[32,40,128]{2,1,0:T(8,128)(2,1)}), s16[32,40,128]{2,1,0:T(8,128)(2,1)S(1)}, u32[]{:S(2)}, u32[]{:S(2)}) %all-to-all-start.4) | async-done | bytes 327712 | tf_op jit(solution)/shard_map/all_to_all | solution.py:295
  115.2 0.0 copy-done.2
  115.2 0.7 last.1
Async XLA Ops:
  2.8 24.3 %all-to-all-start = ((f32[32,2,128]{2,1,0:T(2,128)}), f32[32,2,128]{2,1,0:T(2,128)S(1)}, u32[]{:S(2)}, u32[]{:S(2)}) async-start(f32[32,2,128]{2,1,0:T(2,128)} %stats.1), calls=%async_computation | async-start | bytes 65536 | tf_op jit(solution)/shard_map/all_to_all | solution.py:242
  16.8 1.0 copy-start
  17.8 1.0 copy-start.1
  70.8 44.3 %copy-start.2 = (f32[4096]{0:T(1024)S(1)}, f32[4096]{0:T(1024)}, u32[]{:S(2)}) copy-start(f32[4096]{0:T(1024)} %param.8) | copy-start | bytes 49156
  98.4 16.7 %all-to-all-start.4 = ((s16[32,40,128]{2,1,0:T(8,128)(2,1)}), s16[32,40,128]{2,1,0:T(8,128)(2,1)S(1)}, u32[]{:S(2)}, u32[]{:S(2)}) async-start(s16[32,40,128]{2,1,0:T(8,128)(2,1)} %get-tuple-element.15), calls=%async_computation.4 | async-start | bytes 655360 | tf_op jit(solution)/shard_map/all_to_all | solution.py:295

commit v5 on v4

--- a/solution.py
+++ b/solution.py
@@ -13,6 +13,7 @@
 LANES = 128
 DEPTH = 128
 WIRE_ROWS = 40
+PIECES = 4
 LEAST_POWER = -111.0
 entropy_weight = 0.5
 offset_small = 1e-06
@@ -21,6 +22,7 @@
 BF16 = jnp.bfloat16
 NT_DIMS = (((1,), (1,)), ((), ()))
 VMEM = pl.BlockSpec(memory_space=pltpu.VMEM)
+HBM = pl.BlockSpec(memory_space=pltpu.HBM)
 SMEM = pl.BlockSpec(memory_space=pltpu.SMEM)
 
 
@@ -32,17 +34,25 @@
 
 
 def stats_kernel(peers, x_hbm, y_hbm, out_ref, x_ref, y_ref, sems):
-    copies = [
-        pltpu.make_async_copy(x_hbm, x_ref, sems.at[0]),
-        pltpu.make_async_copy(y_hbm, y_ref, sems.at[1]),
-    ]
-    for copy in copies:
-        copy.start()
+    width = x_ref.shape[1] // PIECES
+    pairs = ((x_hbm, x_ref), (y_hbm, y_ref))
+
+    def piece(which, number):
+        columns = pl.ds(number * width, width)
+        far, near = pairs[which]
+        return pltpu.make_async_copy(
+            far.at[:, columns], near.at[:, columns], sems.at[which, number]
+        )
+
+    for which in range(2):
+        for number in range(PIECES):
+            piece(which, number).start()
     for which, in_ref in enumerate((x_ref, y_ref)):
-        copies[which].wait()
         total = jnp.zeros((PCS, LANES), F32)
         squares = jnp.zeros((PCS, LANES), F32)
         for first in range(0, in_ref.shape[1], LANES):
+            if first % width == 0:
+                piece(which, first // width).wait()
             wide = in_ref[:, first : first + LANES].astype(F32)
             total = total + wide
             squares = squares + wide * wide
@@ -119,7 +129,9 @@
         ).astype(BF16)
 
 
-def row_kernel(peers, k_ref, sums_ref, mass_ref, out_ref, left_ref, line_ref):
+def row_kernel(
+    peers, k_ref, sums_ref, mass_ref, out_hbm, left_ref, line_ref, whole_ref, sems
+):
     spread(left_ref, mass_ref[...] / jnp.sum(sums_ref[...].astype(F32), 0))
     count = k_ref.shape[1]
     block = 512
@@ -130,9 +142,15 @@
         for part in range(0, block, LANES):
             at = (first + part) // LANES
             line_ref[at : at + 1, :] = result[0:1, part : part + LANES]
-    whole = line_ref[...].astype(out_ref.dtype)
-    for peer in range(peers):
-        out_ref[peer] = whole
+    whole_ref[...] = line_ref[...].astype(BF16)
+    copies = [
+        pltpu.make_async_copy(whole_ref, out_hbm.at[peer], sems.at[peer])
+        for peer in range(peers)
+    ]
+    for copy in copies:
+        copy.start()
+    for copy in copies:
+        copy.wait()
 
 
 def col_kernel(peers, k_ref, sums_ref, mass_ref, out_ref, scaling_ref):
@@ -152,7 +170,9 @@
                 out_ref[peer, at : at + 1, :] = line
 
 
-def fate_kernel(k_ref, sums_ref, mass_ref, labels_ref, out_ref, potential_ref, left_ref):
+def fate_kernel(
+    k_ref, sums_ref, mass_ref, labels_ref, out_hbm, potential_ref, left_ref, wire_ref, sems
+):
     scaling = mass_ref[...] / jnp.sum(sums_ref[...], 0)
     potential_ref[...] = entropy_weight * jnp.log(scaling)
     sets = lax.broadcasted_iota(jnp.int32, (SETS, LANES), 0)
@@ -163,6 +183,7 @@
         ).astype(BF16)
     count = k_ref.shape[1]
     block = 512
+    copies = []
     for first in range(0, count, block):
         result = jnp.dot(
             left_ref[...], k_ref[:, first : first + block], preferred_element_type=F32
@@ -174,7 +195,14 @@
             scaled = jnp.minimum(share * jnp.exp2(15.0 - power) + 0.5, 32767.0)
             rest = jnp.broadcast_to(power, (WIRE_ROWS - SETS, LANES))
             coded = jnp.concatenate([scaled, rest], 0).astype(jnp.int32)
-            out_ref[(first + part) // LANES] = coded.astype(jnp.int16)
+            peer = (first + part) // LANES
+            wire_ref[peer] = coded.astype(jnp.int16)
+            copies.append(
+                pltpu.make_async_copy(wire_ref.at[peer], out_hbm.at[peer], sems.at[peer])
+            )
+            copies[-1].start()
+    for copy in copies:
+        copy.wait()
 
 
 def last_kernel(at_ref, sums_ref, mass_ref, fates_ref, potential_ref):
@@ -192,13 +220,13 @@
     return jax.ShapeDtypeStruct(dims, dtype)
 
 
-def call(kernel, name, outs, in_specs, scratch=(), limit=24):
+def call(kernel, name, outs, in_specs, scratch=(), limit=24, out_specs=None):
     return pl.pallas_call(
         kernel,
         name=name,
         out_shape=outs,
         in_specs=in_specs,
-        out_specs=tuple(VMEM for _ in outs) if isinstance(outs, tuple) else VMEM,
+        out_specs=out_specs if out_specs is not None else tuple(VMEM for _ in outs) if isinstance(outs, tuple) else VMEM,
         scratch_shapes=scratch,
         compiler_params=pltpu.CompilerParams(vmem_limit_bytes=limit * 2**20),
     )
@@ -232,11 +260,11 @@
         functools.partial(stats_kernel, col_size),
         "stats",
         shape((col_size, 2, LANES)),
-        [pl.BlockSpec(memory_space=pltpu.HBM)] * 2,
+        [HBM] * 2,
         [
             pltpu.VMEM(x_lines.shape, BF16),
             pltpu.VMEM(y_lines.shape, BF16),
-            pltpu.SemaphoreType.DMA((2,)),
+            pltpu.SemaphoreType.DMA((2, PIECES)),
         ],
     )(x_far, y_far)
     stats = lax.all_to_all(
@@ -267,13 +295,19 @@
     )(xa, ya, stats, scaling)
     k = pltpu.with_memory_space_constraint(k, pltpu.VMEM)
     sums = lax.all_to_all(sums, "row", 0, 0, tiled=True)
-    scratch = [pltpu.VMEM((16, col_count), BF16), pltpu.VMEM((lines_r, LANES), F32)]
+    scratch = [
+        pltpu.VMEM((16, col_count), BF16),
+        pltpu.VMEM((lines_r, LANES), F32),
+        pltpu.VMEM((lines_r, LANES), BF16),
+        pltpu.SemaphoreType.DMA((col_size,)),
+    ]
     sums = call(
         functools.partial(row_kernel, col_size),
         "rows",
         shape((col_size, lines_r, LANES), BF16),
         [VMEM] * 3,
         scratch,
+        out_specs=HBM,
     )(k, sums, target_mass)
     sums = lax.all_to_all(sums, "col", 0, 0, tiled=True)
     scratch = [pltpu.VMEM((lines_r, LANES), F32)]
@@ -290,7 +324,12 @@
         "fate",
         (shape((lines_r, WIRE_ROWS, LANES), jnp.int16), shape((lines_c, LANES))),
         [VMEM] * 4,
-        [pltpu.VMEM((SETS, col_count), BF16)],
+        [
+            pltpu.VMEM((SETS, col_count), BF16),
+            pltpu.VMEM((lines_r, WIRE_ROWS, LANES), jnp.int16),
+            pltpu.SemaphoreType.DMA((lines_r,)),
+        ],
+        out_specs=(HBM, VMEM),
     )(k, sums, target_mass, labels)
     sums = lax.all_to_all(sums, "col", 0, 0, tiled=True)
     at = lax.axis_index("col").astype(jnp.int32).reshape(1)

time: 117 us -> 118 us (level)
  no operation moved by 1% of the time
where the time goes in v5:
time: 118 us; the launch traced here: 117 us
  Pallas kernels  38.5 us (33%)
  blocking collectives  37.4 us (32%)
  waiting for transfers between devices  20.4 us (17%)
  starting transfers between devices  17.9 us (15%)
  local copies, waits for them, and re-layouts  2.08 us (2%)
    all_to_all x2, blocking collectives, on_device(): sums = lax.all_to_all(sums, 'row', 0, 0, tiled=True)  21.4 us
    all_to_all x1, blocking collectives, on_device(): sums = lax.all_to_all(sums, 'col', 0, 0, tiled=True)  16.1 us
    all_to_all x1, starting transfers between devices, on_device(): lax.all_to_all(stats, ('row', 'col'), 0, 0, axis_index_groups=diagonal_gr...  14 us
    all_to_all x1, waiting for transfers between devices, on_device(): sums = lax.all_to_all(sums, 'col', 0, 0, tiled=True)  12.8 us
    pallas_call x1, Pallas kernels, on_device(): call(functools.partial(gen_kernel, row_size, 1.0 / (repeats * row_count *...  12.1 us
    pallas_call x1, Pallas kernels, on_device(): call(fate_kernel, 'fate', (shape((lines_r, WIRE_ROWS, LANES), jnp.int16),...  8.32 us
    pallas_call x1, Pallas kernels, on_device(): call(functools.partial(col_kernel, row_size), 'cols', shape((row_size, li...  8.21 us
    all_to_all x1, waiting for transfers between devices, on_device(): lax.all_to_all(stats, ('row', 'col'), 0, 0, axis_index_groups=diagonal_gr...  7.52 us
  transfers between devices with their start and end apart: 2, of which 2 were waited for; matrix products, arithmetic and copies ran while one was open for 0% of the time, Pallas kernels for 1%

profile of v5, /device:TPU:1, one launch (start us, length us, event | category | flops | bytes accessed | tf_op | source)
XLA Modules:
  0.0 117.0 jit_solution(3391240094113603158)
XLA Ops:
  0.6 2.2 %stats.1 = f32[32,2,128]{2,1,0:T(2,128)} custom-call(bf16[64,4096]{1,0:T(8,128)(2,1)} %bitcast.10, bf16[64,4096]{1,0:T(8,128)(2,1)} %bitcast.12), custom_call_target="tpu_custom_call" | custom-call | tf_op jit(solution)/shard_map/stats/pallas_call | solution.py:259
  2.8 14.0 %all-to-all-start = ((f32[32,2,128]{2,1,0:T(2,128)}), f32[32,2,128]{2,1,0:T(2,128)S(1)}, u32[]{:S(2)}, u32[]{:S(2)}) async-start(f32[32,2,128]{2,1,0:T(2,128)} %stats.1), calls=%async_computation | async-start | bytes 65536 | tf_op jit(solution)/shard_map/all_to_all | solution.py:270
  16.8 0.0 copy-start
  16.8 1.0 copy-done
  17.9 0.0 copy-start.1
  17.9 1.0 copy-done.1
  18.9 0.7 points.1
  19.6 7.5 %all-to-all-done.stats_ref = f32[32,2,128]{2,1,0:T(2,128)S(1)} async-done(((f32[32,2,128]{2,1,0:T(2,128)}), f32[32,2,128]{2,1,0:T(2,128)S(1)}, u32[]{:S(2)}, u32[]{:S(2)}) %all-to-all-start) | async-done | bytes 32800 | tf_op jit(solution)/shard_map/all_to_all | solution.py:270
  27.1 12.1 %gen.1 = (bf16[4096,4096]{1,0:T(8,128)(2,1)S(1)}, bf16[8,32,128]{2,1,0:T(8,128)(2,1)}) custom-call(bf16[4096,128]{1,0:T(8,128)(2,1)S(1)} %get-tuple-element.11.xa_ref, bf16[4096,128]{1,0:T(8,128)(2,1)S(1)} %get-tuple-element.12.ya_ref, f32[32,2,128]{2,1,0:T(2,128)S(1)} %all-to-all-done.stats_ref, f32[32,128]{1,0:T(8,128)} %bitcast.19), custom_call_target="tpu_custom_call" | custom-call | tf_op jit(solution)/shard_map/gen/pallas_call | solution.py:284
  39.2 9.6 %all_to_all.25.sums_ref = bf16[8,32,128]{2,1,0:T(8,128)(2,1)} all-to-all(bf16[8,32,128]{2,1,0:T(8,128)(2,1)} %get-tuple-element.14), channel_id=1, replica_groups=mesh['row'=8,'col'=32] {'row'}, dimensions={0} | all-to-all | bytes 131072 | tf_op jit(solution)/shard_map/all_to_all | solution.py:297
  48.8 6.3 %rows.1 = bf16[32,32,128]{2,1,0:T(8,128)(2,1)} custom-call(bf16[4096,4096]{1,0:T(8,128)(2,1)S(1)} %get-tuple-element.13.k_ref, bf16[8,32,128]{2,1,0:T(8,128)(2,1)} %all_to_all.25.sums_ref, f32[32,128]{1,0:T(8,128)} %bitcast.16), custom_call_target="tpu_custom_call" | custom-call | tf_op jit(solution)/shard_map/rows/pallas_call | solution.py:304
  55.1 16.1 %all_to_all.26.sums_ref = bf16[32,32,128]{2,1,0:T(8,128)(2,1)} all-to-all(bf16[32,32,128]{2,1,0:T(8,128)(2,1)} %rows.1), channel_id=1, replica_groups=mesh['row'=8,'col'=32] {'col'}, dimensions={0} | all-to-all | bytes 524288 | tf_op jit(solution)/shard_map/all_to_all | solution.py:312
  71.2 0.0 copy-start.2
  71.2 8.2 %cols.1 = f32[8,32,128]{2,1,0:T(8,128)} custom-call(bf16[4096,4096]{1,0:T(8,128)(2,1)S(1)} %get-tuple-element.13.k_ref, bf16[32,32,128]{2,1,0:T(8,128)(2,1)} %all_to_all.26.sums_ref, f32[32,128]{1,0:T(8,128)} %bitcast.14), custom_call_target="tpu_custom_call" | custom-call | tf_op jit(solution)/shard_map/cols/pallas_call | solution.py:314
  79.4 11.8 %all_to_all.27.sums_ref = f32[8,32,128]{2,1,0:T(8,128)} all-to-all(f32[8,32,128]{2,1,0:T(8,128)} %cols.1), channel_id=1, replica_groups=mesh['row'=8,'col'=32] {'row'}, dimensions={0} | all-to-all | bytes 262144 | tf_op jit(solution)/shard_map/all_to_all | solution.py:321
  91.2 8.3 %fate.1 = (s16[32,40,128]{2,1,0:T(8,128)(2,1)}, f32[32,128]{1,0:T(8,128)}) custom-call(bf16[4096,4096]{1,0:T(8,128)(2,1)S(1)} %get-tuple-element.13.k_ref, f32[8,32,128]{2,1,0:T(8,128)} %all_to_all.27.sums_ref, f32[32,128]{1,0:T(8,128)} %bitcast.17, s32[32,128]{1,0:T(8,128)} %bitcast.18), custom_call_target="tpu_custom_call" | custom-call | tf_op jit(solution)/shard_map/fate/pallas_call | solution.py:322
  99.5 3.9 %all-to-all-start.4 = ((s16[32,40,128]{2,1,0:T(8,128)(2,1)}), s16[32,40,128]{2,1,0:T(8,128)(2,1)S(1)}, u32[]{:S(2)}, u32[]{:S(2)}) async-start(s16[32,40,128]{2,1,0:T(8,128)(2,1)} %get-tuple-element.15), calls=%async_computation.4 | async-start | bytes 655360 | tf_op jit(solution)/shard_map/all_to_all | solution.py:334
  103.4 12.8 %all-to-all-done.4.sums_ref = s16[32,40,128]{2,1,0:T(8,128)(2,1)S(1)} async-done(((s16[32,40,128]{2,1,0:T(8,128)(2,1)}), s16[32,40,128]{2,1,0:T(8,128)(2,1)S(1)}, u32[]{:S(2)}, u32[]{:S(2)}) %all-to-all-start.4) | async-done | bytes 327712 | tf_op jit(solution)/shard_map/all_to_all | solution.py:334
  116.2 0.0 copy-done.2
  116.2 0.7 last.1
Async XLA Ops:
  2.8 24.3 %all-to-all-start = ((f32[32,2,128]{2,1,0:T(2,128)}), f32[32,2,128]{2,1,0:T(2,128)S(1)}, u32[]{:S(2)}, u32[]{:S(2)}) async-start(f32[32,2,128]{2,1,0:T(2,128)} %stats.1), calls=%async_computation | async-start | bytes 65536 | tf_op jit(solution)/shard_map/all_to_all | solution.py:270
  16.8 1.0 copy-start
  17.9 1.0 copy-start.1
  71.2 45.1 %copy-start.2 = (f32[4096]{0:T(1024)S(1)}, f32[4096]{0:T(1024)}, u32[]{:S(2)}) copy-start(f32[4096]{0:T(1024)} %param.8) | copy-start | bytes 49156
  99.5 16.7 %all-to-all-start.4 = ((s16[32,40,128]{2,1,0:T(8,128)(2,1)}), s16[32,40,128]{2,1,0:T(8,128)(2,1)S(1)}, u32[]{:S(2)}, u32[]{:S(2)}) async-start(s16[32,40,128]{2,1,0:T(8,128)(2,1)} %get-tuple-element.15), calls=%async_computation.4 | async-start | bytes 655360 | tf_op jit(solution)/shard_map/all_to_all | solution.py:334

commit v6 on v4

--- a/solution.py
+++ b/solution.py
@@ -122,7 +122,7 @@
 def row_kernel(peers, k_ref, sums_ref, mass_ref, out_ref, left_ref, line_ref):
     spread(left_ref, mass_ref[...] / jnp.sum(sums_ref[...].astype(F32), 0))
     count = k_ref.shape[1]
-    block = 512
+    block = 1024
     for first in range(0, count, block):
         result = jnp.dot(
             left_ref[...], k_ref[:, first : first + block], preferred_element_type=F32
@@ -162,7 +162,7 @@
             member, scaling[t : t + 1, :], 0.0
         ).astype(BF16)
     count = k_ref.shape[1]
-    block = 512
+    block = 1024
     for first in range(0, count, block):
         result = jnp.dot(
             left_ref[...], k_ref[:, first : first + block], preferred_element_type=F32

time: 117 us -> 117 us (level)
  no operation moved by 1% of the time
where the time goes in v6:
time: 117 us; the launch traced here: 116 us
  Pallas kernels  37.5 us (32%)
  blocking collectives  37.4 us (32%)
  waiting for transfers between devices  20.4 us (17%)
  starting transfers between devices  17.9 us (15%)
  local copies, waits for them, and re-layouts  2.08 us (2%)
    all_to_all x2, blocking collectives, on_device(): sums = lax.all_to_all(sums, 'row', 0, 0, tiled=True)  21.4 us
    all_to_all x1, blocking collectives, on_device(): sums = lax.all_to_all(sums, 'col', 0, 0, tiled=True)  16 us
    all_to_all x1, starting transfers between devices, on_device(): lax.all_to_all(stats, ('row', 'col'), 0, 0, axis_index_groups=diagonal_gr...  14 us
    all_to_all x1, waiting for transfers between devices, on_device(): sums = lax.all_to_all(sums, 'col', 0, 0, tiled=True)  12.8 us
    pallas_call x1, Pallas kernels, on_device(): call(functools.partial(gen_kernel, row_size, 1.0 / (repeats * row_count *...  12.1 us
    pallas_call x1, Pallas kernels, on_device(): call(functools.partial(col_kernel, row_size), 'cols', shape((row_size, li...  8.21 us
    pallas_call x1, Pallas kernels, on_device(): call(fate_kernel, 'fate', (shape((lines_r, WIRE_ROWS, LANES), jnp.int16),...  7.57 us
    all_to_all x1, waiting for transfers between devices, on_device(): lax.all_to_all(stats, ('row', 'col'), 0, 0, axis_index_groups=diagonal_gr...  7.52 us
  transfers between devices with their start and end apart: 2, of which 2 were waited for; matrix products, arithmetic and copies ran while one was open for 0% of the time, Pallas kernels for 1%

profile of v6, /device:TPU:1, one launch (start us, length us, event | category | flops | bytes accessed | tf_op | source)
XLA Modules:
  0.0 115.9 jit_solution(13662966988164991881)
XLA Ops:
  0.6 2.2 %stats.1 = f32[32,2,128]{2,1,0:T(2,128)} custom-call(bf16[64,4096]{1,0:T(8,128)(2,1)} %bitcast.10, bf16[64,4096]{1,0:T(8,128)(2,1)} %bitcast.12), custom_call_target="tpu_custom_call" | custom-call | tf_op jit(solution)/shard_map/stats/pallas_call | solution.py:231
  2.8 14.0 %all-to-all-start = ((f32[32,2,128]{2,1,0:T(2,128)}), f32[32,2,128]{2,1,0:T(2,128)S(1)}, u32[]{:S(2)}, u32[]{:S(2)}) async-start(f32[32,2,128]{2,1,0:T(2,128)} %stats.1), calls=%async_computation | async-start | bytes 65536 | tf_op jit(solution)/shard_map/all_to_all | solution.py:242
  16.8 0.0 copy-start
  16.8 1.0 copy-done
  17.8 0.0 copy-start.1
  17.8 1.0 copy-done.1
  18.9 0.7 points.1
  19.6 7.5 %all-to-all-done.stats_ref = f32[32,2,128]{2,1,0:T(2,128)S(1)} async-done(((f32[32,2,128]{2,1,0:T(2,128)}), f32[32,2,128]{2,1,0:T(2,128)S(1)}, u32[]{:S(2)}, u32[]{:S(2)}) %all-to-all-start) | async-done | bytes 32800 | tf_op jit(solution)/shard_map/all_to_all | solution.py:242
  27.1 12.1 %gen.1 = (bf16[4096,4096]{1,0:T(8,128)(2,1)S(1)}, bf16[8,32,128]{2,1,0:T(8,128)(2,1)}) custom-call(bf16[4096,128]{1,0:T(8,128)(2,1)S(1)} %get-tuple-element.11.xa_ref, bf16[4096,128]{1,0:T(8,128)(2,1)S(1)} %get-tuple-element.12.ya_ref, f32[32,2,128]{2,1,0:T(2,128)S(1)} %all-to-all-done.stats_ref, f32[32,128]{1,0:T(8,128)} %bitcast.19), custom_call_target="tpu_custom_call" | custom-call | tf_op jit(solution)/shard_map/gen/pallas_call | solution.py:256
  39.2 9.6 %all_to_all.25.sums_ref = bf16[8,32,128]{2,1,0:T(8,128)(2,1)} all-to-all(bf16[8,32,128]{2,1,0:T(8,128)(2,1)} %get-tuple-element.14), channel_id=1, replica_groups=mesh['row'=8,'col'=32] {'row'}, dimensions={0} | all-to-all | bytes 131072 | tf_op jit(solution)/shard_map/all_to_all | solution.py:269
  48.8 6.0 %rows.1 = bf16[32,32,128]{2,1,0:T(8,128)(2,1)} custom-call(bf16[4096,4096]{1,0:T(8,128)(2,1)S(1)} %get-tuple-element.13.k_ref, bf16[8,32,128]{2,1,0:T(8,128)(2,1)} %all_to_all.25.sums_ref, f32[32,128]{1,0:T(8,128)} %bitcast.16), custom_call_target="tpu_custom_call" | custom-call | tf_op jit(solution)/shard_map/rows/pallas_call | solution.py:271
  54.8 16.0 %all_to_all.26.sums_ref = bf16[32,32,128]{2,1,0:T(8,128)(2,1)} all-to-all(bf16[32,32,128]{2,1,0:T(8,128)(2,1)} %rows.1), channel_id=1, replica_groups=mesh['row'=8,'col'=32] {'col'}, dimensions={0} | all-to-all | bytes 524288 | tf_op jit(solution)/shard_map/all_to_all | solution.py:278
  70.8 0.0 copy-start.2
  70.8 8.2 %cols.1 = f32[8,32,128]{2,1,0:T(8,128)} custom-call(bf16[4096,4096]{1,0:T(8,128)(2,1)S(1)} %get-tuple-element.13.k_ref, bf16[32,32,128]{2,1,0:T(8,128)(2,1)} %all_to_all.26.sums_ref, f32[32,128]{1,0:T(8,128)} %bitcast.14), custom_call_target="tpu_custom_call" | custom-call | tf_op jit(solution)/shard_map/cols/pallas_call | solution.py:280
  79.0 11.8 %all_to_all.27.sums_ref = f32[8,32,128]{2,1,0:T(8,128)} all-to-all(f32[8,32,128]{2,1,0:T(8,128)} %cols.1), channel_id=1, replica_groups=mesh['row'=8,'col'=32] {'row'}, dimensions={0} | all-to-all | bytes 262144 | tf_op jit(solution)/shard_map/all_to_all | solution.py:287
  90.9 7.6 %fate.1 = (s16[32,40,128]{2,1,0:T(8,128)(2,1)}, f32[32,128]{1,0:T(8,128)}) custom-call(bf16[4096,4096]{1,0:T(8,128)(2,1)S(1)} %get-tuple-element.13.k_ref, f32[8,32,128]{2,1,0:T(8,128)} %all_to_all.27.sums_ref, f32[32,128]{1,0:T(8,128)} %bitcast.17, s32[32,128]{1,0:T(8,128)} %bitcast.18), custom_call_target="tpu_custom_call" | custom-call | tf_op jit(solution)/shard_map/fate/pallas_call | solution.py:288
  98.4 3.9 %all-to-all-start.4 = ((s16[32,40,128]{2,1,0:T(8,128)(2,1)}), s16[32,40,128]{2,1,0:T(8,128)(2,1)S(1)}, u32[]{:S(2)}, u32[]{:S(2)}) async-start(s16[32,40,128]{2,1,0:T(8,128)(2,1)} %get-tuple-element.15), calls=%async_computation.4 | async-start | bytes 655360 | tf_op jit(solution)/shard_map/all_to_all | solution.py:295
  102.3 12.8 %all-to-all-done.4.sums_ref = s16[32,40,128]{2,1,0:T(8,128)(2,1)S(1)} async-done(((s16[32,40,128]{2,1,0:T(8,128)(2,1)}), s16[32,40,128]{2,1,0:T(8,128)(2,1)S(1)}, u32[]{:S(2)}, u32[]{:S(2)}) %all-to-all-start.4) | async-done | bytes 327712 | tf_op jit(solution)/shard_map/all_to_all | solution.py:295
  115.2 0.0 copy-done.2
  115.2 0.7 last.1
Async XLA Ops:
  2.8 24.3 %all-to-all-start = ((f32[32,2,128]{2,1,0:T(2,128)}), f32[32,2,128]{2,1,0:T(2,128)S(1)}, u32[]{:S(2)}, u32[]{:S(2)}) async-start(f32[32,2,128]{2,1,0:T(2,128)} %stats.1), calls=%async_computation | async-start | bytes 65536 | tf_op jit(solution)/shard_map/all_to_all | solution.py:242
  16.8 1.0 copy-start
  17.8 1.0 copy-start.1
  70.8 44.3 %copy-start.2 = (f32[4096]{0:T(1024)S(1)}, f32[4096]{0:T(1024)}, u32[]{:S(2)}) copy-start(f32[4096]{0:T(1024)} %param.8) | copy-start | bytes 49156
  98.4 16.7 %all-to-all-start.4 = ((s16[32,40,128]{2,1,0:T(8,128)(2,1)}), s16[32,40,128]{2,1,0:T(8,128)(2,1)S(1)}, u32[]{:S(2)}, u32[]{:S(2)}) async-start(s16[32,40,128]{2,1,0:T(8,128)(2,1)} %get-tuple-element.15), calls=%async_computation.4 | async-start | bytes 655360 | tf_op jit(solution)/shard_map/all_to_all | solution.py:295
